TPU v7x, 512 devices: a whole 4x8x8 slice. The times are simulated.
512 devices in a mesh: sector: 32 (over z_hi, x, core), dof: 16 (over z_lo, y).
Axes of the slice: x: 4, y: 8, z: 8 (z_hi: 4, z_lo: 2; z = z_hi * 2 + z_lo), core: 2. Of those that a mesh axis runs over, the one named last changes fastest.
Arguments:
- rhs: float32 [32, 4096, 128], P('sector', 'dof')
- diagonal: float32 [32, 4096], P('sector', 'dof'), may hold values from 4 to 8
- coupling: bfloat16 [32, 4096, 2048], P('sector', 'dof'), may hold values from -0.125 to 0.125
- springs: float32 [32, 3072], P('sector', 'dof'), may hold values from 1 to 4
- precond: bfloat16 [4096, 4096], P('dof')
- hub_inverse: bfloat16 [3072, 3072], P('dof')
Outputs:
- solution: float32 [32, 4096, 128], P('sector', 'dof')
- residual: float32 [32, 4096, 128], P('sector', 'dof')
All inputs are finite; a program needn't handle non-finite values.
Results may differ from a plain program's by a relative error of at most 0.0056.
Values may be sent and summed in bfloat16 or wider, within the bound.
A program may use at most 64 MiB of HBM per device.

v0:
```python
import jax
import jax.numpy as jnp
from jax import lax
from jax.sharding import PartitionSpec as P

ITERS = 3


def extended(cells, sides, width):
    for axis, dim in sides:
        count = lax.axis_size(axis)
        head = lax.slice_in_dim(cells, 0, width, axis=dim)
        tail = lax.slice_in_dim(cells, cells.shape[dim] - width, cells.shape[dim], axis=dim)
        cells = jnp.concatenate(
            [
                lax.ppermute(tail, axis, [(i, (i + 1) % count) for i in range(count)]),
                cells,
                lax.ppermute(head, axis, [((i + 1) % count, i) for i in range(count)]),
            ],
            axis=dim,
        )
    return cells


def fold_rows(field, update, start_value):
    return update(start_value, lax.all_gather(field, "dof", axis=0, tiled=True), jnp.int32(0))


def product_with(matrix):

    def update(total, piece, start):
        return jnp.dot(matrix, piece, preferred_element_type=jnp.float32)

    return update


def place_rows(total, piece, start):
    return piece


def body(rhs, diagonal, coupling, springs, precond, hub_inverse):
    residual = rhs[0]
    diag_rows = diagonal[0]
    couple_rows = coupling[0]
    spring_rows = springs[0][:, None]
    rows_dev = residual.shape[0]
    loads = residual.shape[1]
    quarter = rows_dev // 4
    parts = lax.axis_size("dof")
    solution = jnp.zeros_like(residual)
    for step in range(ITERS):
        precon = fold_rows(
            residual.astype(jnp.bfloat16),
            product_with(precond),
            jnp.zeros((rows_dev, loads), jnp.float32),
        )
        precon_low = precon.astype(jnp.bfloat16)
        own_faces = precon_low[: 2 * quarter]
        whole = fold_rows(
            own_faces, place_rows, jnp.zeros((parts * 2 * quarter, loads), jnp.bfloat16)
        )
        beside_all = extended(whole[None], (("sector", 0),), 1)
        prev_side = beside_all[0].reshape(parts, 2, quarter, loads)[:, 1]
        next_side = beside_all[2].reshape(parts, 2, quarter, loads)[:, 0]
        needed = jnp.stack([prev_side, next_side], axis=1).reshape(parts * 2 * quarter, loads)
        couple = jnp.dot(couple_rows, needed, preferred_element_type=jnp.float32)
        attached = precon[: 3 * quarter]
        load = lax.psum(spring_rows * attached, "sector")
        hub = fold_rows(
            load.astype(jnp.bfloat16),
            product_with(hub_inverse),
            jnp.zeros((3 * quarter, loads), jnp.float32),
        )
        hub_term = jnp.concatenate(
            [spring_rows * (attached - hub), jnp.zeros((quarter, loads), jnp.float32)], axis=0
        )
        image = diag_rows[:, None] * precon + couple + hub_term
        upper, lower = lax.psum(
            (jnp.sum(image * residual, axis=0), jnp.sum(image * image, axis=0)), ("sector", "dof")
        )
        alpha = upper / (lower + 1e-06)
        solution = solution + alpha * precon
        residual = residual - alpha * image
    return (solution[None], residual[None])


def solution(mesh):
    placed = (
        P("sector", "dof", None),
        P("sector", "dof"),
        P("sector", "dof", None),
        P("sector", "dof"),
        P("dof", None),
        P("dof", None),
    )
    return jax.shard_map(
        body,
        mesh=mesh,
        in_specs=placed,
        out_specs=(P("sector", "dof", None), P("sector", "dof", None)),
        check_vma=False,
    )
```

profile of v0, /device:TPU:1, one launch (start us, length us, event | category | flops | bytes accessed | tf_op | source)
XLA Modules:
  0.0 1211.0 jit_solution(1387459577958328483)
XLA Ops:
  7.2 0.0 copy-start
  7.2 0.0 all-gather.4.cloned.1.call-start
  7.2 1.7 bitcast_convert_fusion
  8.9 0.0 all-gather.4.cloned.1.call-update
  8.9 0.0 copy-start.1
  9.0 0.0 all-gather.6.cloned.1.call-start
  9.0 68.9 %all-gather.4.cloned.1.call-done = bf16[4096,128]{1,0:T(8,128)(2,1)} async-done(((bf16[256,128]{1,0:T(8,128)(2,1)}), bf16[4096,128]{1,0:T(8,128)(2,1)}) %all-gather.4.cloned.1.call-update) | async-done | bytes 1048592 | tf_op jit(solution)/shard_map/all_gather | solution.py:26
  77.9 1.9 fusion.18
  79.8 30.4 %all_gather.28 = bf16[2048,128]{1,0:T(8,128)(2,1)} all-gather(bf16[128,128]{1,0:T(8,128)(2,1)S(1)} %slice.71), channel_id=1, replica_groups=mesh['sector'=32,'dof'=16] {'dof'}, dimensions={0}, use_global_device_ids=true | all-gather | bytes 557056 | tf_op jit(solution)/shard_map/all_gather | solution.py:26
  110.2 19.7 %collective-permute-start.1 = (bf16[1,2048,128]{2,1,0:T(8,128)(2,1)}, bf16[1,2048,128]{2,1,0:T(8,128)(2,1)}, u32[]{:S(2)}, u32[]{:S(2)}) collective-permute-start(bf16[1,2048,128]{2,1,0:T(8,128)(2,1)} %bitcast.2), channel_id=1, source_target_pairs={{16,0},{32,16},{48,32},{64,48},{80,64},{96,80},{112,96},{128,112},... | collective-permute-start | bytes 1572872 | tf_op jit(solution)/shard_map/ppermute | solution.py:18
  129.9 3.0 collective-permute-start
  132.9 0.1 slice_multiply_fusion.2
  133.0 139.5 %psum.63 = bf16[192,128]{1,0:T(8,128)(2,1)} all-reduce(f32[192,128]{1,0:T(8,128)S(1)} %slice_multiply_fusion.2), channel_id=1, replica_groups=mesh['sector'=32,'dof'=16] {'sector'}, use_global_device_ids=true, to_apply=%region_0.0 | all-reduce | flops 24576 | bytes 147456 | tf_op jit(solution)/shard_map/psum | solution.py:68
  272.6 28.3 %all_gather.29 = bf16[3072,128]{1,0:T(8,128)(2,1)S(1)} all-gather(bf16[192,128]{1,0:T(8,128)(2,1)} %psum.63), channel_id=1, replica_groups=mesh['sector'=32,'dof'=16] {'dof'}, dimensions={0}, use_global_device_ids=true | all-gather | bytes 835584 | tf_op jit(solution)/shard_map/all_gather | solution.py:26
  300.8 0.0 copy-start.13
  300.9 0.5 fusion.11
  301.3 0.0 collective-permute-done.1
  301.4 1.0 slice.50
  302.3 0.0 collective-permute-done
  302.3 1.0 slice.49
  303.3 0.1 pad_maximum_fusion
  303.4 1.1 multiply_reduce_fusion.4
  304.5 108.3 %all-reduce.5 = (f32[128]{0:T(128)}, f32[128]{0:T(128)}) all-reduce(f32[128]{0:T(128)S(1)} %get-tuple-element.7, f32[128]{0:T(128)S(1)} %get-tuple-element.6), channel_id=1, replica_groups=mesh['sector'=32,'dof'=16] {'sector','dof'}, use_global_device_ids=true, to_apply=%region_2.0 | all-reduce | flops 256 | bytes 2048 | tf_op jit(solution)/shard_map/psum | solution.py:78
  412.8 0.7 add_divide_fusion.2
  413.5 1.6 fusion.17
  415.1 0.0 all-gather.6.cloned.1.call-update
  415.1 0.0 all-gather.8.cloned.1.call-start
  415.2 56.7 %all-gather.6.cloned.1.call-done = bf16[4096,128]{1,0:T(8,128)(2,1)} async-done(((bf16[256,128]{1,0:T(8,128)(2,1)}), bf16[4096,128]{1,0:T(8,128)(2,1)}) %all-gather.6.cloned.1.call-update) | async-done | bytes 1048592 | tf_op jit(solution)/shard_map/all_gather | solution.py:26
  471.8 1.9 convolution_bitcast_fusion.1
  473.8 0.7 slice_multiply_fusion.1
  474.5 30.4 %all_gather.31 = bf16[2048,128]{1,0:T(8,128)(2,1)} all-gather(bf16[128,128]{1,0:T(8,128)(2,1)S(1)} %slice.70), channel_id=1, replica_groups=mesh['sector'=32,'dof'=16] {'dof'}, dimensions={0}, use_global_device_ids=true | all-gather | bytes 557056 | tf_op jit(solution)/shard_map/all_gather | solution.py:26
  504.9 19.7 %collective-permute-start.3 = (bf16[1,2048,128]{2,1,0:T(8,128)(2,1)}, bf16[1,2048,128]{2,1,0:T(8,128)(2,1)}, u32[]{:S(2)}, u32[]{:S(2)}) collective-permute-start(bf16[1,2048,128]{2,1,0:T(8,128)(2,1)} %bitcast.11), channel_id=1, source_target_pairs={{16,0},{32,16},{48,32},{64,48},{80,64},{96,80},{112,96},{128,112},... | collective-permute-start | bytes 1572872 | tf_op jit(solution)/shard_map/ppermute | solution.py:18
  524.6 3.0 collective-permute-start.2
  527.6 139.7 %psum.66 = bf16[192,128]{1,0:T(8,128)(2,1)} all-reduce(f32[192,128]{1,0:T(8,128)} %slice_multiply_fusion.1), channel_id=1, replica_groups=mesh['sector'=32,'dof'=16] {'sector'}, use_global_device_ids=true, to_apply=%region_5.0 | all-reduce | flops 24576 | bytes 147456 | tf_op jit(solution)/shard_map/psum | solution.py:68
  667.2 28.3 %all_gather.32 = bf16[3072,128]{1,0:T(8,128)(2,1)S(1)} all-gather(bf16[192,128]{1,0:T(8,128)(2,1)} %psum.66), channel_id=1, replica_groups=mesh['sector'=32,'dof'=16] {'dof'}, dimensions={0}, use_global_device_ids=true | all-gather | bytes 835584 | tf_op jit(solution)/shard_map/all_gather | solution.py:26
  695.5 0.5 fusion.9
  696.0 0.0 collective-permute-done.3
  696.0 1.0 slice.54
  697.0 1.0 slice.53
  698.0 0.1 pad_maximum_fusion.1
  698.0 1.7 multiply_reduce_fusion.2
  699.7 108.3 %all-reduce.4 = (f32[128]{0:T(128)}, f32[128]{0:T(128)}) all-reduce(f32[128]{0:T(128)} %get-tuple-element.5, f32[128]{0:T(128)S(1)} %get-tuple-element.4), channel_id=1, replica_groups=mesh['sector'=32,'dof'=16] {'sector','dof'}, use_global_device_ids=true, to_apply=%region_7.0 | all-reduce | flops 256 | bytes 2048 | tf_op jit(solution)/shard_map/psum | solution.py:78
  808.1 0.6 add_divide_fusion.1
  808.7 1.7 fusion.16
  810.3 0.0 all-gather.8.cloned.1.call-update
  810.4 56.7 %all-gather.8.cloned.1.call-done = bf16[4096,128]{1,0:T(8,128)(2,1)} async-done(((bf16[256,128]{1,0:T(8,128)(2,1)}), bf16[4096,128]{1,0:T(8,128)(2,1)}) %all-gather.8.cloned.1.call-update) | async-done | bytes 1048592 | tf_op jit(solution)/shard_map/all_gather | solution.py:26
  867.0 1.9 convolution_bitcast_fusion
  869.0 0.0 copy-start.5
  869.0 0.6 copy-done.5
  869.6 0.7 slice_multiply_fusion
  870.4 30.4 %all_gather.34 = bf16[2048,128]{1,0:T(8,128)(2,1)} all-gather(bf16[128,128]{1,0:T(8,128)(2,1)S(1)} %slice.69), channel_id=1, replica_groups=mesh['sector'=32,'dof'=16] {'dof'}, dimensions={0}, use_global_device_ids=true | all-gather | bytes 557056 | tf_op jit(solution)/shard_map/all_gather | solution.py:26
  900.7 19.7 %collective-permute-start.5 = (bf16[1,2048,128]{2,1,0:T(8,128)(2,1)}, bf16[1,2048,128]{2,1,0:T(8,128)(2,1)}, u32[]{:S(2)}, u32[]{:S(2)}) collective-permute-start(bf16[1,2048,128]{2,1,0:T(8,128)(2,1)} %bitcast.18), channel_id=1, source_target_pairs={{16,0},{32,16},{48,32},{64,48},{80,64},{96,80},{112,96},{128,112},... | collective-permute-start | bytes 1572872 | tf_op jit(solution)/shard_map/ppermute | solution.py:18
  920.4 3.0 collective-permute-start.4
  923.4 139.7 %psum.69 = bf16[192,128]{1,0:T(8,128)(2,1)} all-reduce(f32[192,128]{1,0:T(8,128)} %slice_multiply_fusion), channel_id=1, replica_groups=mesh['sector'=32,'dof'=16] {'sector'}, use_global_device_ids=true, to_apply=%region_10.0 | all-reduce | flops 24576 | bytes 147456 | tf_op jit(solution)/shard_map/psum | solution.py:68
  1063.1 28.3 %all_gather.35 = bf16[3072,128]{1,0:T(8,128)(2,1)S(1)} all-gather(bf16[192,128]{1,0:T(8,128)(2,1)} %psum.69), channel_id=1, replica_groups=mesh['sector'=32,'dof'=16] {'dof'}, dimensions={0}, use_global_device_ids=true | all-gather | bytes 835584 | tf_op jit(solution)/shard_map/all_gather | solution.py:26
  1091.4 1.5 fusion.7
  1092.8 0.0 copy-start.7
  1092.9 0.0 copy-start.10
  1092.9 1.0 slice.58
  1093.9 1.0 slice.57
  1094.9 0.1 pad_maximum_fusion.2
  1095.0 0.5 multiply_reduce_fusion
  1095.4 108.3 %all-reduce.3 = (f32[128]{0:T(128)S(1)}, f32[128]{0:T(128)S(1)}) all-reduce(f32[128]{0:T(128)S(1)} %get-tuple-element.3, f32[128]{0:T(128)S(1)} %get-tuple-element.2), channel_id=1, replica_groups=mesh['sector'=32,'dof'=16] {'sector','dof'}, use_global_device_ids=true, to_apply=%region_12.0 | all-reduce | flops 256 | bytes 2048 | tf_op jit(solution)/shard_map/psum | solution.py:78
  1203.8 0.7 subtract_bitcast_fusion
  (28 shorter events, 0.1 us)
Async XLA Ops:
  7.2 70.7 %copy-start = (bf16[256,4096]{1,0:T(8,128)(2,1)S(1)}, bf16[256,4096]{1,0:T(8,128)(2,1)}, u32[]{:S(2)}) copy-start(bf16[256,4096]{1,0:T(8,128)(2,1)} %param.10) | copy-start | bytes 6291460
  7.2 125.7 %copy-start.12 = (f32[1,192]{1,0:T(1,128)S(1)}, f32[1,192]{1,0:T(1,128)}, u32[]{:S(2)}) copy-start(f32[1,192]{1,0:T(1,128)} %param.9) | copy-start | bytes 2308
  7.2 70.7 %all-gather.4.cloned.1.call-start = ((), (), s32[]{:S(2)}) async-start(), calls=%async_computation | async-start | bytes 1114112 | tf_op jit(solution)/shard_map/all_gather | solution.py:26
  8.9 291.9 %copy-start.1 = (bf16[192,3072]{1,0:T(8,128)(2,1)S(1)}, bf16[192,3072]{1,0:T(8,128)(2,1)}, u32[]{:S(2)}) copy-start(bf16[192,3072]{1,0:T(8,128)(2,1)} %param.11) | copy-start | bytes 3538948
  9.0 462.9 %all-gather.6.cloned.1.call-start = ((), (), s32[]{:S(2)}) async-start(), calls=%async_computation.1 | async-start | bytes 1114112 | tf_op jit(solution)/shard_map/all_gather | solution.py:26
  110.2 191.1 %collective-permute-start.1 = (bf16[1,2048,128]{2,1,0:T(8,128)(2,1)}, bf16[1,2048,128]{2,1,0:T(8,128)(2,1)}, u32[]{:S(2)}, u32[]{:S(2)}) collective-permute-start(bf16[1,2048,128]{2,1,0:T(8,128)(2,1)} %bitcast.2), channel_id=1, source_target_pairs={{16,0},{32,16},{48,32},{64,48},{80,64},{96,80},{112,96},{128,112},... | collective-permute-start | bytes 1572872 | tf_op jit(solution)/shard_map/ppermute | solution.py:18
  129.9 172.4 %collective-permute-start = (bf16[1,2048,128]{2,1,0:T(8,128)(2,1)}, bf16[1,2048,128]{2,1,0:T(8,128)(2,1)}, u32[]{:S(2)}, u32[]{:S(2)}) collective-permute-start(bf16[1,2048,128]{2,1,0:T(8,128)(2,1)} %bitcast.2), channel_id=1, source_target_pairs={{0,16},{16,32},{32,48},{48,64},{64,80},{80,96},{96,112},{112,128},... | collective-permute-start | bytes 1572872 | tf_op jit(solution)/shard_map/ppermute | solution.py:16
  300.8 2.5 copy-start.2
  300.8 2.6 copy-start.8
  300.8 2.6 copy-start.13
  415.1 451.9 %all-gather.8.cloned.1.call-start = ((), (), s32[]{:S(2)}) async-start(), calls=%async_computation.2 | async-start | bytes 1114112 | tf_op jit(solution)/shard_map/all_gather | solution.py:26
  504.9 191.1 %collective-permute-start.3 = (bf16[1,2048,128]{2,1,0:T(8,128)(2,1)}, bf16[1,2048,128]{2,1,0:T(8,128)(2,1)}, u32[]{:S(2)}, u32[]{:S(2)}) collective-permute-start(bf16[1,2048,128]{2,1,0:T(8,128)(2,1)} %bitcast.11), channel_id=1, source_target_pairs={{16,0},{32,16},{48,32},{64,48},{80,64},{96,80},{112,96},{128,112},... | collective-permute-start | bytes 1572872 | tf_op jit(solution)/shard_map/ppermute | solution.py:18
  524.6 172.4 %collective-permute-start.2 = (bf16[1,2048,128]{2,1,0:T(8,128)(2,1)}, bf16[1,2048,128]{2,1,0:T(8,128)(2,1)}, u32[]{:S(2)}, u32[]{:S(2)}) collective-permute-start(bf16[1,2048,128]{2,1,0:T(8,128)(2,1)} %bitcast.11), channel_id=1, source_target_pairs={{0,16},{16,32},{32,48},{48,64},{64,80},{80,96},{96,112},{112,128},... | collective-permute-start | bytes 1572872 | tf_op jit(solution)/shard_map/ppermute | solution.py:16
  695.5 2.5 copy-start.3
  695.5 2.5 copy-start.11
  869.0 0.7 copy-start.5
  900.7 192.1 %collective-permute-start.5 = (bf16[1,2048,128]{2,1,0:T(8,128)(2,1)}, bf16[1,2048,128]{2,1,0:T(8,128)(2,1)}, u32[]{:S(2)}, u32[]{:S(2)}) collective-permute-start(bf16[1,2048,128]{2,1,0:T(8,128)(2,1)} %bitcast.18), channel_id=1, source_target_pairs={{16,0},{32,16},{48,32},{64,48},{80,64},{96,80},{112,96},{128,112},... | collective-permute-start | bytes 1572872 | tf_op jit(solution)/shard_map/ppermute | solution.py:18
  920.4 173.5 %collective-permute-start.4 = (bf16[1,2048,128]{2,1,0:T(8,128)(2,1)}, bf16[1,2048,128]{2,1,0:T(8,128)(2,1)}, u32[]{:S(2)}, u32[]{:S(2)}) collective-permute-start(bf16[1,2048,128]{2,1,0:T(8,128)(2,1)} %bitcast.18), channel_id=1, source_target_pairs={{0,16},{16,32},{32,48},{48,64},{64,80},{80,96},{96,112},{112,128},... | collective-permute-start | bytes 1572872 | tf_op jit(solution)/shard_map/ppermute | solution.py:16
  1091.4 3.6 copy-start.4
  1091.4 3.6 copy-start.6
  1091.4 3.6 copy-start.9
  1092.8 110.9 %copy-start.7 = (f32[256,128]{1,0:T(8,128)S(1)}, f32[256,128]{1,0:T(8,128)}, u32[]{:S(2)}) copy-start(f32[256,128]{1,0:T(8,128)} %copy-done.5) | copy-start | bytes 393220
  1092.9 110.9 %copy-start.10 = (f32[256,128]{1,0:T(8,128)S(1)}, f32[256,128]{1,0:T(8,128)}, u32[]{:S(2)}) copy-start(f32[256,128]{1,0:T(8,128)} %get-tuple-element.15) | copy-start | bytes 393220
Sparse Core Ops, SparseCore 0:
  10.7 67.1 all-gather.3
  415.3 56.5 all-gather.5
  810.5 56.5 all-gather.7
where the time goes:
time: 1210 us
  blocking collectives  920 us (76%)
  waiting for transfers between devices  182 us (15%)
  starting transfers between devices  68.2 us (6%)
  between operations  14.1 us (1%)
    psum x3, blocking collectives, body(): load = lax.psum(spring_rows * attached, 'sector')  419 us
    psum x3, blocking collectives, body(): lax.psum((jnp.sum(image * residual, axis=0), jnp.sum(image * image, axis=...  325 us
    all_gather x3, waiting for transfers between devices, fold_rows(): lax.all_gather(field, 'dof', axis=0, tiled=True)  182 us
    all_gather x6, blocking collectives, fold_rows(): lax.all_gather(field, 'dof', axis=0, tiled=True)  176 us
    ppermute x3, starting transfers between devices, extended(): lax.ppermute(head, axis, [((i + 1) % count, i) for i in range(count)])  59 us
  transfers between devices with their start and end apart: 9, of which 3 were waited for; matrix products, arithmetic and copies ran while one was open for 0% of the time, Pallas kernels for 0%

commit v1 on v0

v1 whole, which is shorter than its diff:
```python
import jax
import jax.numpy as jnp
from jax import lax
from jax.experimental import pallas as pl
from jax.experimental.pallas import tpu as pltpu
from jax.sharding import PartitionSpec as P

ITERS = 3
NY, NZL, NZH, NG = 8, 2, 4, 8
PARTS = NY * NZL
QUARTER = 64
ROWS = 4 * QUARTER
FACE = 2 * QUARTER
ATT = 3 * QUARTER
PIECE = ATT // NG
LOADS = 128
MESH = pl.DeviceIdType.MESH

OWN_SENDS = (("r", 0), ("l", 1), ("z", 2))
EVENTS = (
    (0, -1, (("r", 3), ("z", 5))),
    (0, 1, (("l", 4), ("z", 6))),
    (1, 0, ()),
    (0, -2, (("r", 7), ("z", 9))),
    (0, 2, (("l", 8), ("z", 10))),
    (1, -1, ()),
    (1, 1, ()),
    (0, -3, (("r", 11),)),
    (0, 3, ()),
    (1, -2, (("r", 12),)),
    (1, 2, (("l", 13),)),
    (0, -4, ()),
    (1, -3, ()),
    (1, 3, (("l", 14),)),
    (1, 4, ()),
)


def kernel(
    rhs_ref, diag_ref, spring_ref, couple_hbm, pre_hbm, hub_hbm, sol_ref, res_ref,
    pre, coup, hubraw, hubblk, rbuf, fbuf, lbuf, stage, v, acc, cacc, hacc, main, spr,
    part, rs_recv, zsrc, zrecv, asrc, agbuf, dsrc, drecv,
    load_sem, r_send, r_recv, f_send, f_recv, l_send, l_recv, x_send, x_recv,
    rs_send, rs_sem, z_send, z_sem, a_send, a_sem, d_send, d_sem,
):
    s = lax.axis_index("sector")
    d = lax.axis_index("dof")
    zh, g = s // NG, s % NG
    zl, y = d // NY, d % NY
    z = zh * NZL + zl
    nsec = NZH * NG

    def dof_at(column, offset):
        col = zl if column == 0 else 1 - zl
        return col * NY + (y + offset + NY) % NY

    link_dev = {
        "r": (s, dof_at(0, 1)),
        "l": (s, dof_at(0, -1)),
        "z": (s, dof_at(1, 0)),
    }
    y_peer = [(s, zl * NY + (y + j) % NY) for j in range(NY)]
    z_all = [(z + j) % (NZH * NZL) for j in range(NZH * NZL)]
    z_peer = [((zz // NZL) * NG + g, (zz % NZL) * NY + y) for zz in z_all]
    g_index = [(g + j) % NG for j in range(NG)]
    g_peer = [(zh * NG + gg, d) for gg in g_index]
    zh_peer = [(((zh + k) % NZH) * NG + g, d) for k in range(NZH)]
    next_sec = ((s + 1) % nsec, d)
    prev_sec = ((s + nsec - 1) % nsec, d)

    def send(src, dst, ssem, rsem, dev):
        pltpu.make_async_remote_copy(
            src_ref=src, dst_ref=dst, send_sem=ssem, recv_sem=rsem,
            device_id=dev, device_id_type=MESH,
        ).start()

    def arrived(ref, sem):
        pltpu.make_async_copy(ref, ref, sem).wait()

    loads_in = [
        pltpu.make_async_copy(pre_hbm, pre, load_sem.at[0]),
        pltpu.make_async_copy(hub_hbm, hubraw, load_sem.at[1]),
        pltpu.make_async_copy(couple_hbm.at[0], coup, load_sem.at[2]),
    ]
    for c in loads_in:
        c.start()

    barrier = pltpu.get_barrier_semaphore()
    greet = y_peer[1:] + z_peer[1:] + g_peer[1:] + [next_sec, prev_sec]
    for dev in greet:
        pl.semaphore_signal(barrier, inc=1, device_id=dev, device_id_type=MESH)

    res_ref[0] = rhs_ref[0]
    rbuf[d] = rhs_ref[0].astype(jnp.bfloat16)
    sol_ref[0] = jnp.zeros((ROWS, LOADS), jnp.float32)
    sp = jnp.broadcast_to(spring_ref[...], (LOADS, ATT)).T
    spr[...] = sp
    main[...] = jnp.broadcast_to(diag_ref[...], (LOADS, ROWS)).T
    main[:ATT] = main[:ATT] + sp
    dsrc[...] = jnp.zeros(dsrc.shape, jnp.float32)
    pl.semaphore_wait(barrier, len(greet))

    def begin_gather(buf, ssem, rsem):
        for link, there in OWN_SENDS:
            send(buf.at[d], buf.at[d], ssem, rsem.at[there], link_dev[link])

    def take(buf, ssem, rsem, event):
        column, offset, onward = EVENTS[event]
        idx = dof_at(column, offset)
        arrived(buf.at[idx], rsem.at[event])
        for link, there in onward:
            send(buf.at[idx], buf.at[idx], ssem, rsem.at[there], link_dev[link])
        return idx

    begin_gather(rbuf, r_send, r_recv)

    loads_in[1].wait()
    for j in range(PARTS):
        hubblk[j] = hubraw[:, j * ATT:(j + 1) * ATT]
    loads_in[0].wait()
    loads_in[2].wait()

    def pre_dot(idx):
        off = pl.multiple_of(idx * ROWS, ROWS)
        return jnp.dot(pre[:, pl.ds(off, ROWS)], rbuf[idx], preferred_element_type=jnp.float32)

    def couple_dot(idx):
        off = pl.multiple_of(idx * FACE, FACE)
        return jnp.dot(coup[:, pl.ds(off, FACE)], fbuf[idx], preferred_element_type=jnp.float32)

    def hub_dot(idx):
        return jnp.dot(hubblk[idx], lbuf[idx], preferred_element_type=jnp.float32)

    def step(it, carry):
        acc[...] = pre_dot(d)
        for e in range(len(EVENTS)):
            idx = take(rbuf, r_send, r_recv, e)
            acc[...] += pre_dot(idx)
        v[...] = acc[...]
        part[...] = (spr[...] * v[:ATT]).reshape(NG, PIECE, LOADS)
        for j in range(1, NG):
            send(part.at[g_index[j]], rs_recv.at[j], rs_send, rs_sem.at[j], g_peer[j])
        stage[...] = v[:FACE].astype(jnp.bfloat16)
        send(stage.at[pl.ds(QUARTER, QUARTER)], fbuf.at[d, pl.ds(0, QUARTER)], x_send, x_recv.at[0], next_sec)
        send(stage.at[pl.ds(0, QUARTER)], fbuf.at[d, pl.ds(QUARTER, QUARTER)], x_send, x_recv.at[1], prev_sec)
        total = part[g]
        for j in range(1, NG):
            arrived(rs_recv.at[j], rs_sem.at[j])
            total = total + rs_recv[j]
        zsrc[...] = total
        for k in range(1, NZH):
            send(zsrc, zrecv.at[k], z_send, z_sem.at[k], zh_peer[k])
        arrived(fbuf.at[d, pl.ds(0, QUARTER)], x_recv.at[0])
        arrived(fbuf.at[d, pl.ds(QUARTER, QUARTER)], x_recv.at[1])
        begin_gather(fbuf, f_send, f_recv)
        cacc[...] = couple_dot(d)

        def face(e):
            idx = take(fbuf, f_send, f_recv, e)
            cacc[...] += couple_dot(idx)

        def load(e):
            idx = take(lbuf, l_send, l_recv, e)
            hacc[...] += hub_dot(idx)

        for k in range(1, NZH):
            arrived(zrecv.at[k], z_sem.at[k])
            total = total + zrecv[k]
        asrc[...] = total
        for j in range(1, NG):
            send(asrc, agbuf.at[g], a_send, a_sem.at[j], g_peer[j])
        agbuf[g] = total
        for e in range(0, 3):
            face(e)
        for j in range(1, NG):
            arrived(agbuf.at[(g + NG - j) % NG], a_sem.at[j])
        lbuf[d] = agbuf[...].reshape(ATT, LOADS).astype(jnp.bfloat16)
        begin_gather(lbuf, l_send, l_recv)
        hacc[...] = hub_dot(d)
        for e in range(3, 7):
            face(e)
        for e in range(0, 3):
            load(e)
        for e in range(7, 11):
            face(e)
        for e in range(3, 7):
            load(e)
        for e in range(11, 15):
            face(e)
        for e in range(7, 15):
            load(e)

        acc[...] = main[...] * v[...] + cacc[...]
        acc[:ATT] = acc[:ATT] - spr[...] * hacc[...]
        arrived(rbuf.at[pl.ds(0, 15)], r_send)
        arrived(fbuf.at[pl.ds(0, 15)], f_send)
        arrived(lbuf.at[pl.ds(0, 15)], l_send)
        arrived(stage, x_send)
        arrived(part.at[pl.ds(0, NG - 1)], rs_send)
        arrived(part.at[pl.ds(0, NZH - 1)], z_send)
        arrived(part.at[pl.ds(0, NG - 1)], a_send)
        image = acc[...]
        up = jnp.sum(image * res_ref[0], axis=0, keepdims=True)
        low = jnp.sum(image * image, axis=0, keepdims=True)
        dsrc[0, 0:1] = up
        dsrc[0, 1:2] = low
        for p, peers in enumerate((y_peer, z_peer, g_peer)):
            for j in range(1, 8):
                send(dsrc.at[p], drecv.at[p, j], d_send.at[p], d_sem.at[p, j], peers[j])
            total = dsrc[p]
            for j in range(1, 8):
                arrived(drecv.at[p, j], d_sem.at[p, j])
                total = total + drecv[p, j]
            dsrc[p + 1] = total
        alpha = dsrc[3, 0:1] / (dsrc[3, 1:2] + 1e-06)
        res = res_ref[0] - alpha * acc[...]
        for p in range(3):
            arrived(drecv.at[p, pl.ds(0, 7)], d_send.at[p])

        @pl.when(it < ITERS - 1)
        def _():
            rbuf[d] = res.astype(jnp.bfloat16)
            begin_gather(rbuf, r_send, r_recv)

        res_ref[0] = res
        sol_ref[0] = sol_ref[0] + alpha * v[...]
        return carry

    lax.fori_loop(0, ITERS, step, 0)


def body(rhs, diagonal, coupling, springs, precond, hub_inverse):
    vm = pl.BlockSpec(memory_space=pltpu.VMEM)
    hbm = pl.BlockSpec(memory_space=pl.ANY)
    f32, bf16 = jnp.float32, jnp.bfloat16
    dma = pltpu.SemaphoreType.DMA
    n = len(EVENTS)
    return pl.pallas_call(
        kernel,
        out_shape=(
            jax.ShapeDtypeStruct((1, ROWS, LOADS), f32),
            jax.ShapeDtypeStruct((1, ROWS, LOADS), f32),
        ),
        in_specs=[vm, vm, vm, hbm, hbm, hbm],
        out_specs=(vm, vm),
        scratch_shapes=[
            pltpu.VMEM((ROWS, PARTS * ROWS), bf16),
            pltpu.VMEM((ROWS, PARTS * FACE), bf16),
            pltpu.VMEM((ATT, PARTS * ATT), bf16),
            pltpu.VMEM((PARTS, ATT, ATT), bf16),
            pltpu.VMEM((PARTS, ROWS, LOADS), bf16),
            pltpu.VMEM((PARTS, FACE, LOADS), bf16),
            pltpu.VMEM((PARTS, ATT, LOADS), bf16),
            pltpu.VMEM((FACE, LOADS), bf16),
            pltpu.VMEM((ROWS, LOADS), f32),
            pltpu.VMEM((ROWS, LOADS), f32),
            pltpu.VMEM((ROWS, LOADS), f32),
            pltpu.VMEM((ATT, LOADS), f32),
            pltpu.VMEM((ROWS, LOADS), f32),
            pltpu.VMEM((ATT, LOADS), f32),
            pltpu.VMEM((NG, PIECE, LOADS), f32),
            pltpu.VMEM((NG, PIECE, LOADS), f32),
            pltpu.VMEM((PIECE, LOADS), f32),
            pltpu.VMEM((NZH, PIECE, LOADS), f32),
            pltpu.VMEM((PIECE, LOADS), f32),
            pltpu.VMEM((NG, PIECE, LOADS), f32),
            pltpu.VMEM((4, 8, LOADS), f32),
            pltpu.VMEM((3, 8, 8, LOADS), f32),
            dma((3,)),
            dma, dma((n,)),
            dma, dma((n,)),
            dma, dma((n,)),
            dma, dma((2,)),
            dma, dma((NG,)),
            dma, dma((NZH,)),
            dma, dma((NG,)),
            dma((3,)), dma((3, 8)),
        ],
        compiler_params=pltpu.CompilerParams(
            collective_id=0, has_side_effects=True, vmem_limit_bytes=40 * 1024 * 1024
        ),
    )(rhs, diagonal, springs, coupling, precond, hub_inverse)


def solution(mesh):
    placed = (
        P("sector", "dof", None),
        P("sector", "dof"),
        P("sector", "dof", None),
        P("sector", "dof"),
        P("dof", None),
        P("dof", None),
    )
    return jax.shard_map(
        body,
        mesh=mesh,
        in_specs=placed,
        out_specs=(P("sector", "dof", None), P("sector", "dof", None)),
        check_vma=False,
    )
```

time: 1210 us -> 221 us (0.18)
  blocking collectives: 920 us -> 0 us
  Pallas kernels: 0 us -> 212 us
  waiting for transfers between devices: 182 us -> 0 us
  starting transfers between devices: 68.2 us -> 0 us
  between operations: 14.1 us -> 0.65 us
    psum x6 -> x0, blocking collectives: 744 us -> none  [the longest x3 419 us: body(): load = lax.psum(spring_rows * attached, 'sector')]
    pallas_call x0 -> x1, Pallas kernels: none -> 212 us  [body(): pl.pallas_call(kernel, out_shape=(jax.ShapeDtypeStruct((1, ROWS, LOADS),...]
    all_gather x3 -> x0, waiting for transfers between devices: 182 us -> none  [fold_rows(): lax.all_gather(field, 'dof', axis=0, tiled=True)]
    all_gather x6 -> x0, blocking collectives: 176 us -> none  [fold_rows(): lax.all_gather(field, 'dof', axis=0, tiled=True)]
    ppermute x6 -> x0, starting transfers between devices: 68 us -> none  [the longest x3 59 us: extended(): lax.ppermute(head, axis, [((i + 1) % count, i) for i in range(count)])]
  transfers between devices with their start and end apart: 9 -> 0, of which waited for: 3 -> 0; matrix products, arithmetic and copies ran while one was open for 0% -> 0% of each run, Pallas kernels for 0% -> 0%
where the time goes in v1:
time: 221 us; the launch traced here: 220 us
  Pallas kernels  212 us (96%)
  local copies, waits for them, and re-layouts  7.65 us (3%)
    pallas_call x1, Pallas kernels, body(): pl.pallas_call(kernel, out_shape=(jax.ShapeDtypeStruct((1, ROWS, LOADS),...  212 us
    unnamed x14, local copies, waits for them, and re-layouts  7.65 us

profile of v1, /device:TPU:1, one launch (start us, length us, event | category | flops | bytes accessed | tf_op | source)
XLA Modules:
  0.0 220.5 jit_solution(15119642884561836767)
XLA Ops:
  0.6 0.0 copy-start
  0.6 1.6 copy-done
  2.2 0.0 copy-start.1
  2.2 1.3 copy-done.1
  3.5 0.0 copy-start.2
  3.5 1.2 copy-done.2
  4.7 0.0 copy-start.3
  4.7 0.9 copy-done.3
  5.6 0.0 copy-start.4
  5.6 0.7 copy-done.4
  6.3 0.0 copy-start.5
  6.3 0.7 copy-done.5
  7.0 212.2 %shard_map.77 = (f32[1,256,128]{2,1,0:T(8,128)S(1)}, f32[1,256,128]{2,1,0:T(8,128)S(1)}) custom-call(f32[1,256,128]{2,1,0:T(8,128)S(1)} %copy-done.3, f32[1,256]{1,0:T(1,128)S(1)} %copy-done.4, f32[1,192]{1,0:T(1,128)S(1)} %copy-done.5, bf16[1,256,2048]{2,1,0:T(8,128)(2,1)S(1)} %copy-done.2, bf16[256,4096]{1,0:T(8,128)(2,1)S(1)} %copy-done, ...), custom_call_target="tpu_custom_call" | custom-call | tf_op jit(solution)/shard_map/pallas_call | solution.py:238
  219.1 0.7 copy.10
  219.8 0.7 copy.11
Async XLA Ops:
  0.6 1.6 copy-start
  2.2 1.3 copy-start.1
  3.5 1.2 copy-start.2
  4.7 0.9 copy-start.3
  5.6 0.7 copy-start.4
  6.3 0.7 copy-start.5

commit v2 on v0

v2 whole, which is shorter than its diff:
```python
import jax
import jax.numpy as jnp
from jax import lax
from jax.experimental import pallas as pl
from jax.experimental.pallas import tpu as pltpu
from jax.sharding import PartitionSpec as P

ITERS = 3
NX, NY, NZL, NZH = 4, 8, 2, 4
NZ = NZL * NZH
PARTS = NY * NZL
QUARTER = 64
ROWS = 4 * QUARTER
FACE = 2 * QUARTER
ATT = 3 * QUARTER
HALF = ATT // 2
LOADS = 128
MESH = pl.DeviceIdType.MESH

NEAR = (-1, 1, -2, 2, -3, 3, 4)
COLUMN = len(NEAR)
BLOCKS = 2 * COLUMN + 1


def kernel(
    rhs_ref, diag_ref, spring_ref, couple_hbm, pre_hbm, hub_hbm, sol_ref, res_ref,
    pre, coup, hubraw, hubblk, rbuf, fbuf, lbuf, qold, qnew, stage, v, acc, cacc, hacc, hrecv,
    main, spr, csend, crecv, xsend, xrecv, zsend, zrecv, dsrc, dof_dots, pair_src, pair_dots, all_dots,
    load_sem, r_send, r_sem, f_send, f_sem, n_send, n_sem, c_send, c_sem, x_send, x_sem,
    z_send, z_sem, y_send, y_sem, h_send, h_sem, d_send, d_sem, p_send, p_sem, a_send, a_sem,
):
    s = lax.axis_index("sector")
    d = lax.axis_index("dof")
    zh, x, c = s // (2 * NX), (s // 2) % NX, s % 2
    zl, y = d // NY, d % NY
    z = zh * NZL + zl
    plane = zh * NX + x
    nsec = NZH * NX * 2

    def sector_of(zh, x, c):
        return (zh * NX + x) * 2 + c

    def dof_at(column, offset):
        col = zl if column == 0 else 1 - zl
        return col * NY + (y + offset + NY) % NY

    y_peer = [(s, zl * NY + (y + j) % NY) for j in range(NY)]
    z_at = [(z + j) % NZ for j in range(NZ)]
    z_peer = [(sector_of(zz // NZL, x, c), (zz % NZL) * NY + y) for zz in z_at]
    x_peer = [(sector_of(zh, (x + j) % NX, c), d) for j in range(NX)]
    dof_peer = [(s, (d + j) % PARTS) for j in range(PARTS)]
    plane_at = [(plane + j) % (NZH * NX) for j in range(NZH * NX)]
    plane_peer = [(m * 2 + c, d) for m in plane_at]
    partner = (s, dof_at(1, 0))
    sibling = (sector_of(zh, x, 1 - c), d)
    next_sec = ((s + 1) % nsec, d)
    prev_sec = ((s + nsec - 1) % nsec, d)

    def send(src, dst, ssem, rsem, dev):
        pltpu.make_async_remote_copy(
            src_ref=src, dst_ref=dst, send_sem=ssem, recv_sem=rsem,
            device_id=dev, device_id_type=MESH,
        ).start()

    def arrived(ref, sem):
        pltpu.make_async_copy(ref, ref, sem).wait()

    loads_in = [
        pltpu.make_async_copy(pre_hbm, pre, load_sem.at[0]),
        pltpu.make_async_copy(hub_hbm, hubraw, load_sem.at[1]),
        pltpu.make_async_copy(couple_hbm.at[0], coup, load_sem.at[2]),
    ]
    for copy in loads_in:
        copy.start()

    barrier = pltpu.get_barrier_semaphore()
    greet = dof_peer[1:] + plane_peer[1:] + z_peer[1::2] + [sibling, next_sec, prev_sec]
    for dev in greet:
        pl.semaphore_signal(barrier, inc=1, device_id=dev, device_id_type=MESH)

    res_ref[0] = rhs_ref[0]
    rbuf[d] = rhs_ref[0].astype(jnp.bfloat16)
    sol_ref[0] = jnp.zeros((ROWS, LOADS), jnp.float32)
    sp = jnp.broadcast_to(spring_ref[...], (LOADS, ATT)).T
    spr[...] = sp
    main[...] = jnp.broadcast_to(diag_ref[...], (LOADS, ROWS)).T
    main[:ATT] = main[:ATT] + sp
    dsrc[...] = jnp.zeros(dsrc.shape, jnp.float32)
    pl.semaphore_wait(barrier, len(greet))

    def begin_gather(buf, ssem, rsem):
        for k, offset in enumerate(NEAR):
            send(buf.at[d], buf.at[d], ssem, rsem.at[k], (s, dof_at(0, -offset)))
        send(buf.at[d], buf.at[d], ssem, rsem.at[COLUMN], partner)

    def take(buf, ssem, rsem, event):
        if event < COLUMN:
            idx = dof_at(0, NEAR[event])
        elif event == COLUMN:
            idx = dof_at(1, 0)
        else:
            idx = dof_at(1, NEAR[event - COLUMN - 1])
        arrived(buf.at[idx], rsem.at[event])
        if event < COLUMN:
            send(buf.at[idx], buf.at[idx], ssem, rsem.at[COLUMN + 1 + event], partner)
        return idx

    def pre_dot(idx):
        off = pl.multiple_of(idx * ROWS, ROWS)
        return jnp.dot(pre[:, pl.ds(off, ROWS)], rbuf[idx], preferred_element_type=jnp.float32)

    def couple_dot(idx):
        off = pl.multiple_of(idx * FACE, FACE)
        return jnp.dot(coup[:, pl.ds(off, FACE)], fbuf[idx], preferred_element_type=jnp.float32)

    def hub_dot(idx):
        rows = lbuf[idx].reshape(ATT, LOADS)
        return jnp.dot(hubblk[idx], rows, preferred_element_type=jnp.float32)

    def ratio(squares, low):
        return jnp.clip(jnp.sqrt(squares / jnp.maximum(low, 1e-30)), 1e-12, 1e12)

    def image_of_v():
        other = pl.multiple_of((1 - c) * HALF, 8)
        mine = pl.multiple_of(c * HALF, 8)
        csend[...] = spr[pl.ds(other, HALF)] * v[pl.ds(other, HALF)]
        send(csend, crecv, c_send, c_sem, sibling)
        stage[...] = v[:FACE].astype(jnp.bfloat16)
        right, left = pl.ds(QUARTER, QUARTER), pl.ds(0, QUARTER)
        send(stage.at[right], fbuf.at[d, left], n_send, n_sem.at[0], next_sec)
        send(stage.at[left], fbuf.at[d, right], n_send, n_sem.at[1], prev_sec)
        part = spr[pl.ds(mine, HALF)] * v[pl.ds(mine, HALF)]
        arrived(crecv, c_sem)
        part = part + crecv[...]
        xsend[...] = part
        for j in range(1, NX):
            send(xsend, xrecv.at[j], x_send, x_sem.at[j], x_peer[j])
        arrived(fbuf.at[d, left], n_sem.at[0])
        arrived(fbuf.at[d, right], n_sem.at[1])
        begin_gather(fbuf, f_send, f_sem)
        for j in range(1, NX):
            arrived(xrecv.at[j], x_sem.at[j])
            part = part + xrecv[j]
        zsend[...] = part.astype(jnp.bfloat16)
        for j in range(1, NZ):
            send(zsend, zrecv.at[j], z_send, z_sem.at[j], z_peer[j])
        cacc[...] = couple_dot(d)

        def face(event):
            cacc[...] += couple_dot(take(fbuf, f_send, f_sem, event))

        for event in range(COLUMN):
            face(event)
        across = jnp.zeros((HALF, LOADS), jnp.float32)
        for j in range(1, NZ):
            arrived(zrecv.at[j], z_sem.at[j])
            term = zrecv[j].astype(jnp.float32)
            if j % 2 == 0:
                part = part + term
            else:
                across = across + term
        lbuf[y, zl] = part.astype(jnp.bfloat16)
        lbuf[y, 1 - zl] = across.astype(jnp.bfloat16)
        for j in range(1, NY):
            send(lbuf.at[y], lbuf.at[y], y_send, y_sem.at[j], y_peer[j])
        hacc[...] = hub_dot(y)
        for event in range(COLUMN, BLOCKS):
            face(event)
        acc[...] = main[...] * v[...] + cacc[...]
        for j in range(1, NY):
            idx = (y + NY - j) % NY
            arrived(lbuf.at[idx], y_sem.at[j])
            hacc[...] += hub_dot(idx)
        send(hacc, hrecv, h_send, h_sem, sibling)
        arrived(csend, c_send)
        arrived(stage, n_send)
        arrived(xrecv.at[pl.ds(0, NX - 1)], x_send)
        arrived(fbuf.at[pl.ds(0, BLOCKS)], f_send)
        arrived(zrecv.at[pl.ds(0, NZ - 1)], z_send)
        arrived(lbuf.at[pl.ds(0, NY - 1)], y_send)
        arrived(hrecv, h_sem)
        acc[:ATT] = acc[:ATT] - spr[...] * (hacc[...] + hrecv[...])
        arrived(hacc, h_send)

    def column_sum(a):
        return jnp.sum(a, axis=0, keepdims=True)

    def dots_begin():
        for j in range(1, PARTS):
            send(dsrc, dof_dots.at[d], d_send, d_sem.at[j], dof_peer[j])
        dof_dots[d] = dsrc[...]

    def dots_pair():
        for j in range(1, PARTS):
            arrived(dof_dots.at[(d + PARTS - j) % PARTS], d_sem.at[j])
        pair_src[...] = jnp.sum(dof_dots[...], axis=0)
        send(pair_src, pair_dots, p_send, p_sem, sibling)

    def dots_plane():
        arrived(pair_dots, p_sem)
        all_dots[plane] = pair_src[...] + pair_dots[...]
        for j in range(1, NZH * NX):
            send(all_dots.at[plane], all_dots.at[plane], a_send, a_sem.at[j], plane_peer[j])

    def dots_end():
        for j in range(1, NZH * NX):
            arrived(all_dots.at[(plane + NZH * NX - j) % (NZH * NX)], a_sem.at[j])
        total = jnp.sum(all_dots[...], axis=0)
        arrived(dof_dots.at[pl.ds(0, PARTS - 1)], d_send)
        arrived(pair_src, p_send)
        arrived(all_dots.at[pl.ds(0, NZH * NX - 1)], a_send)
        return total[0:1] / (total[1:2] + 1e-06)

    def local_dots():
        image, res = acc[...], res_ref[0]
        low, squares = column_sum(image * image), column_sum(res * res)
        dsrc[0:1] = column_sum(image * res)
        dsrc[1:2] = low
        dsrc[2:3] = squares
        return ratio(squares, low)

    def advance(alpha):
        sol_ref[0] = sol_ref[0] + alpha * v[...]
        res_ref[0] = res_ref[0] - alpha * acc[...]

    begin_gather(rbuf, r_send, r_sem)
    loads_in[1].wait()
    for core in range(2):
        @pl.when(c == core)
        def _():
            for k in range(NY):
                for col in range(NZL):
                    at = (col * NY + k) * ATT + core * HALF
                    hubblk[k, :, col * HALF:(col + 1) * HALF] = hubraw[:, at:at + HALF]
    loads_in[0].wait()
    loads_in[2].wait()
    qold[d] = pre_dot(d)
    for event in range(BLOCKS):
        idx = take(rbuf, r_send, r_sem, event)
        qold[idx] = pre_dot(idx)
    total = qold[0]
    for k in range(1, PARTS):
        total = total + qold[k]
    v[...] = total
    arrived(rbuf.at[pl.ds(0, BLOCKS)], r_send)

    def step(it, carry):
        image_of_v()
        trial = local_dots()
        rbuf[d] = (res_ref[0] - trial * acc[...]).astype(jnp.bfloat16)
        begin_gather(rbuf, r_send, r_sem)
        dots_begin()
        qnew[d] = pre_dot(d)

        def block(event):
            idx = take(rbuf, r_send, r_sem, event)
            qnew[idx] = pre_dot(idx)

        for event in range(COLUMN):
            block(event)
        dots_pair()
        block(COLUMN)
        block(COLUMN + 1)
        dots_plane()
        for event in range(COLUMN + 2, BLOCKS):
            block(event)
        alpha = dots_end()
        arrived(rbuf.at[pl.ds(0, BLOCKS)], r_send)
        advance(alpha)
        total = jnp.zeros((ROWS, LOADS), jnp.float32)
        for k in range(PARTS):
            grow = alpha / ratio(dof_dots[k, 2:3], dof_dots[k, 1:2])
            q = grow * qnew[k] - (grow - 1.0) * qold[k]
            qold[k] = q
            total = total + q
        v[...] = total
        return carry

    lax.fori_loop(0, ITERS - 1, step, 0)
    image_of_v()
    local_dots()
    dots_begin()
    dots_pair()
    dots_plane()
    advance(dots_end())


def body(rhs, diagonal, coupling, springs, precond, hub_inverse):
    vm = pl.BlockSpec(memory_space=pltpu.VMEM)
    hbm = pl.BlockSpec(memory_space=pl.ANY)
    f32, bf16 = jnp.float32, jnp.bfloat16
    dma = pltpu.SemaphoreType.DMA
    mem = pltpu.VMEM
    return pl.pallas_call(
        kernel,
        out_shape=(
            jax.ShapeDtypeStruct((1, ROWS, LOADS), f32),
            jax.ShapeDtypeStruct((1, ROWS, LOADS), f32),
        ),
        in_specs=[vm, vm, vm, hbm, hbm, hbm],
        out_specs=(vm, vm),
        scratch_shapes=[
            mem((ROWS, PARTS * ROWS), bf16),
            mem((ROWS, PARTS * FACE), bf16),
            mem((ATT, PARTS * ATT), bf16),
            mem((NY, ATT, ATT), bf16),
            mem((PARTS, ROWS, LOADS), bf16),
            mem((PARTS, FACE, LOADS), bf16),
            mem((NY, NZL, HALF, LOADS), bf16),
            mem((PARTS, ROWS, LOADS), f32),
            mem((PARTS, ROWS, LOADS), f32),
            mem((FACE, LOADS), bf16),
            mem((ROWS, LOADS), f32),
            mem((ROWS, LOADS), f32),
            mem((ROWS, LOADS), f32),
            mem((ATT, LOADS), f32),
            mem((ATT, LOADS), f32),
            mem((ROWS, LOADS), f32),
            mem((ATT, LOADS), f32),
            mem((HALF, LOADS), f32),
            mem((HALF, LOADS), f32),
            mem((HALF, LOADS), f32),
            mem((NX, HALF, LOADS), f32),
            mem((HALF, LOADS), bf16),
            mem((NZ, HALF, LOADS), bf16),
            mem((8, LOADS), f32),
            mem((PARTS, 8, LOADS), f32),
            mem((8, LOADS), f32),
            mem((8, LOADS), f32),
            mem((NZH * NX, 8, LOADS), f32),
            dma((3,)),
            dma, dma((BLOCKS,)),
            dma, dma((BLOCKS,)),
            dma, dma((2,)),
            dma, dma,
            dma, dma((NX,)),
            dma, dma((NZ,)),
            dma, dma((NY,)),
            dma, dma,
            dma, dma((PARTS,)),
            dma, dma,
            dma, dma((NZH * NX,)),
        ],
        compiler_params=pltpu.CompilerParams(
            collective_id=0, has_side_effects=True, vmem_limit_bytes=40 * 1024 * 1024
        ),
    )(rhs, diagonal, springs, coupling, precond, hub_inverse)


def solution(mesh):
    placed = (
        P("sector", "dof", None),
        P("sector", "dof"),
        P("sector", "dof", None),
        P("sector", "dof"),
        P("dof", None),
        P("dof", None),
    )
    return jax.shard_map(
        body,
        mesh=mesh,
        in_specs=placed,
        out_specs=(P("sector", "dof", None), P("sector", "dof", None)),
        check_vma=False,
    )
```

time: 1210 us -> 184 us (0.15)
  blocking collectives: 920 us -> 0 us
  waiting for transfers between devices: 182 us -> 0 us
  Pallas kernels: 0 us -> 175 us
  starting transfers between devices: 68.2 us -> 0 us
  between operations: 14.1 us -> 0.65 us
    psum x6 -> x0, blocking collectives: 744 us -> none  [the longest x3 419 us: body(): load = lax.psum(spring_rows * attached, 'sector')]
    all_gather x3 -> x0, waiting for transfers between devices: 182 us -> none  [fold_rows(): lax.all_gather(field, 'dof', axis=0, tiled=True)]
    all_gather x6 -> x0, blocking collectives: 176 us -> none  [fold_rows(): lax.all_gather(field, 'dof', axis=0, tiled=True)]
    pallas_call x0 -> x1, Pallas kernels: none -> 175 us  [body(): pl.pallas_call(kernel, out_shape=(jax.ShapeDtypeStruct((1, ROWS, LOADS),...]
    ppermute x6 -> x0, starting transfers between devices: 68 us -> none  [the longest x3 59 us: extended(): lax.ppermute(head, axis, [((i + 1) % count, i) for i in range(count)])]
  transfers between devices with their start and end apart: 9 -> 0, of which waited for: 3 -> 0; matrix products, arithmetic and copies ran while one was open for 0% -> 0% of each run, Pallas kernels for 0% -> 0%
where the time goes in v2:
time: 184 us; the launch traced here: 183 us
  Pallas kernels  175 us (95%)
  local copies, waits for them, and re-layouts  7.65 us (4%)
    pallas_call x1, Pallas kernels, body(): pl.pallas_call(kernel, out_shape=(jax.ShapeDtypeStruct((1, ROWS, LOADS),...  175 us
    unnamed x14, local copies, waits for them, and re-layouts  7.65 us

profile of v2, /device:TPU:1, one launch (start us, length us, event | category | flops | bytes accessed | tf_op | source)
XLA Modules:
  0.0 183.2 jit_solution(9048640012437980177)
XLA Ops:
  0.6 0.0 copy-start
  0.6 1.6 copy-done
  2.2 0.0 copy-start.1
  2.2 1.3 copy-done.1
  3.5 0.0 copy-start.2
  3.5 1.2 copy-done.2
  4.7 0.0 copy-start.3
  4.7 0.9 copy-done.3
  5.6 0.0 copy-start.4
  5.6 0.7 copy-done.4
  6.3 0.0 copy-start.5
  6.3 0.7 copy-done.5
  7.0 174.9 %shard_map.77 = (f32[1,256,128]{2,1,0:T(8,128)S(1)}, f32[1,256,128]{2,1,0:T(8,128)S(1)}) custom-call(f32[1,256,128]{2,1,0:T(8,128)S(1)} %copy-done.3, f32[1,256]{1,0:T(1,128)S(1)} %copy-done.4, f32[1,192]{1,0:T(1,128)S(1)} %copy-done.5, bf16[1,256,2048]{2,1,0:T(8,128)(2,1)S(1)} %copy-done.2, bf16[256,4096]{1,0:T(8,128)(2,1)S(1)} %copy-done, ...), custom_call_target="tpu_custom_call" | custom-call | tf_op jit(solution)/shard_map/pallas_call | solution.py:294
  181.9 0.7 copy.10
  182.6 0.7 copy.11
Async XLA Ops:
  0.6 1.6 copy-start
  2.2 1.3 copy-start.1
  3.5 1.2 copy-start.2
  4.7 0.9 copy-start.3
  5.6 0.7 copy-start.4
  6.3 0.7 copy-start.5

commit v3 on v2

v3 whole, which is shorter than its diff:
```python
import jax
import jax.numpy as jnp
from jax import lax
from jax.experimental import pallas as pl
from jax.experimental.pallas import tpu as pltpu
from jax.sharding import PartitionSpec as P

ITERS = 3
NX, NY, NZL, NZH = 4, 8, 2, 4
NZ = NZL * NZH
PARTS = NY * NZL
QUARTER = 64
ROWS = 4 * QUARTER
FACE = 2 * QUARTER
ATT = 3 * QUARTER
HALF = ATT // 2
LOADS = 128
MESH = pl.DeviceIdType.MESH

NEAR = (-1, 1, -2, 2, -3, 3, 4)
COLUMN = len(NEAR)
BLOCKS = 2 * COLUMN + 1


def kernel(
    rhs_hbm, diag_hbm, spring_hbm, couple_hbm, pre_hbm, hub_hbm, sol_ref, res_ref,
    diag_row, spring_row, pre, coup, hubraw, hubblk, rbuf, fbuf, lbuf, qold, qnew, stage,
    v, vec, image, acc, cacc, hacc, hrecv, main, spr, csend, crecv, xsend, xrecv, zsend, zrecv, dsrc, dof_dots, pair_src, pair_dots, all_dots,
    load_sem, r_send, r_sem, f_send, f_sem, n_send, n_sem, c_send, c_sem, x_send, x_sem,
    z_send, z_sem, y_send, y_sem, h_send, h_sem, d_send, d_sem, p_send, p_sem, a_send, a_sem,
):
    s = lax.axis_index("sector")
    d = lax.axis_index("dof")
    zh, x, c = s // (2 * NX), (s // 2) % NX, s % 2
    zl, y = d // NY, d % NY
    z = zh * NZL + zl
    plane = zh * NX + x
    nsec = NZH * NX * 2

    def sector_of(zh, x, c):
        return (zh * NX + x) * 2 + c

    def dof_at(column, offset):
        col = zl if column == 0 else 1 - zl
        return col * NY + (y + offset + NY) % NY

    y_peer = [(s, zl * NY + (y + j) % NY) for j in range(NY)]
    z_at = [(z + j) % NZ for j in range(NZ)]
    z_peer = [(sector_of(zz // NZL, x, c), (zz % NZL) * NY + y) for zz in z_at]
    x_peer = [(sector_of(zh, (x + j) % NX, c), d) for j in range(NX)]
    dof_peer = [(s, (d + j) % PARTS) for j in range(PARTS)]
    plane_at = [(plane + j) % (NZH * NX) for j in range(NZH * NX)]
    plane_peer = [(m * 2 + c, d) for m in plane_at]
    partner = (s, dof_at(1, 0))
    sibling = (sector_of(zh, x, 1 - c), d)
    next_sec = ((s + 1) % nsec, d)
    prev_sec = ((s + nsec - 1) % nsec, d)

    def send(src, dst, ssem, rsem, dev):
        pltpu.make_async_remote_copy(
            src_ref=src, dst_ref=dst, send_sem=ssem, recv_sem=rsem,
            device_id=dev, device_id_type=MESH,
        ).start()

    def arrived(ref, sem):
        pltpu.make_async_copy(ref, ref, sem).wait()

    loads_in = [
        pltpu.make_async_copy(rhs_hbm, res_ref, load_sem.at[0]),
        pltpu.make_async_copy(pre_hbm, pre, load_sem.at[1]),
        pltpu.make_async_copy(diag_hbm, diag_row, load_sem.at[2]),
        pltpu.make_async_copy(spring_hbm, spring_row, load_sem.at[3]),
        pltpu.make_async_copy(hub_hbm, hubraw, load_sem.at[4]),
        pltpu.make_async_copy(couple_hbm.at[0], coup, load_sem.at[5]),
    ]
    for copy in loads_in:
        copy.start()

    barrier = pltpu.get_barrier_semaphore()
    greet = dof_peer[1:] + plane_peer[1:] + z_peer[1::2] + [sibling, next_sec, prev_sec]
    for dev in greet:
        pl.semaphore_signal(barrier, inc=1, device_id=dev, device_id_type=MESH)

    loads_in[0].wait()
    rbuf[d] = res_ref[0].astype(jnp.bfloat16)
    pl.semaphore_wait(barrier, len(greet))

    def begin_gather(buf, ssem, rsem):
        for k, offset in enumerate(NEAR):
            send(buf.at[d], buf.at[d], ssem, rsem.at[k], (s, dof_at(0, -offset)))
        send(buf.at[d], buf.at[d], ssem, rsem.at[COLUMN], partner)

    def take(buf, ssem, rsem, event):
        idx = dof_at(0, NEAR[event])
        arrived(buf.at[idx], rsem.at[event])
        send(buf.at[idx], buf.at[idx], ssem, rsem.at[COLUMN], partner)
        return idx

    across_first = (1 - zl) * NY

    def take_across(buf, rsem):
        arrived(buf.at[pl.ds(across_first, NY)], rsem.at[COLUMN])

    def pre_dot(idx):
        off = pl.multiple_of(idx * ROWS, ROWS)
        return jnp.dot(pre[:, pl.ds(off, ROWS)], rbuf[idx], preferred_element_type=jnp.float32)

    def couple_dot(faces, first, count):
        off = pl.multiple_of(first * FACE, FACE)
        rows = faces[pl.ds(first, count)].reshape(count * FACE, LOADS)
        return jnp.dot(coup[:, pl.ds(off, count * FACE)], rows, preferred_element_type=jnp.float32)

    def ratio(squares, low):
        return jnp.clip(jnp.sqrt(squares / jnp.maximum(low, 1e-30)), 1e-12, 1e12)

    def apply_operator(turn, late):
        faces = fbuf.at[turn]
        other = pl.multiple_of((1 - c) * HALF, 8)
        mine = pl.multiple_of(c * HALF, 8)
        csend[...] = spr[pl.ds(other, HALF)] * vec[pl.ds(other, HALF)]
        send(csend, crecv, c_send, c_sem, sibling)
        stage[...] = vec[:FACE].astype(jnp.bfloat16)
        right, left = pl.ds(QUARTER, QUARTER), pl.ds(0, QUARTER)
        send(stage.at[right], faces.at[d, left], n_send, n_sem.at[turn, 0], next_sec)
        send(stage.at[left], faces.at[d, right], n_send, n_sem.at[turn, 1], prev_sec)
        part = spr[pl.ds(mine, HALF)] * vec[pl.ds(mine, HALF)]
        arrived(crecv, c_sem)
        part = part + crecv[...]
        xsend[...] = part
        for j in range(1, NX):
            send(xsend, xrecv.at[turn, j], x_send, x_sem.at[turn], x_peer[j])
        arrived(faces.at[d, left], n_sem.at[turn, 0])
        arrived(faces.at[d, right], n_sem.at[turn, 1])
        begin_gather(faces, f_send, f_sem)
        arrived(xrecv.at[turn, pl.ds(1, NX - 1)], x_sem.at[turn])
        part = part + xrecv[turn, 1] + xrecv[turn, 2] + xrecv[turn, 3]
        zsend[...] = part.astype(jnp.bfloat16)
        for j in range(1, NZ):
            send(zsend, zrecv.at[turn, j], z_send, z_sem.at[turn], z_peer[j])
        cacc[...] = couple_dot(faces, d, 1)
        for event in range(COLUMN):
            cacc[...] += couple_dot(faces, take(faces, f_send, f_sem, event), 1)
        arrived(zrecv.at[turn, pl.ds(1, NZ - 1)], z_sem.at[turn])
        across = zrecv[turn, 1].astype(jnp.float32)
        for j in range(2, NZ):
            term = zrecv[turn, j].astype(jnp.float32)
            if j % 2 == 0:
                part = part + term
            else:
                across = across + term
        lbuf[y, zl] = part.astype(jnp.bfloat16)
        lbuf[y, 1 - zl] = across.astype(jnp.bfloat16)
        for j in range(1, NY):
            send(lbuf.at[y], lbuf.at[y], y_send, y_sem, y_peer[j])
        take_across(faces, f_sem)
        acc[...] = main[...] * vec[...] + cacc[...] + couple_dot(faces, across_first, NY)
        late()
        arrived(csend, c_send)
        arrived(stage, n_send)
        arrived(xrecv.at[turn, pl.ds(0, NX - 1)], x_send)
        arrived(faces.at[pl.ds(0, BLOCKS)], f_send)
        arrived(zrecv.at[turn, pl.ds(0, NZ - 1)], z_send)
        arrived(lbuf.at[pl.ds(0, NY - 1)], y_send)
        arrived(lbuf.at[pl.ds(0, NY - 1)], y_sem)
        rows = lbuf[...].reshape(NY * ATT, LOADS)
        hacc[...] = jnp.dot(hubblk[...], rows, preferred_element_type=jnp.float32)
        send(hacc, hrecv, h_send, h_sem, sibling)
        arrived(hrecv, h_sem)
        acc[:ATT] = acc[:ATT] - spr[...] * (hacc[...] + hrecv[...])
        arrived(hacc, h_send)

    def column_sum(a):
        return jnp.sum(a, axis=0, keepdims=True)

    def dots_begin():
        for j in range(1, PARTS):
            send(dsrc, dof_dots.at[d], d_send, d_sem, dof_peer[j])
        dof_dots[d] = dsrc[...]

    def dots_pair():
        arrived(dof_dots.at[pl.ds(0, PARTS - 1)], d_sem)
        pair_src[...] = jnp.sum(dof_dots[...], axis=0)
        send(pair_src, pair_dots, p_send, p_sem, sibling)

    def dots_plane(turn):
        arrived(pair_dots, p_sem)
        dots = all_dots.at[turn]
        dots[plane] = pair_src[...] + pair_dots[...]
        for j in range(1, NZH * NX):
            send(dots.at[plane], dots.at[plane], a_send, a_sem.at[turn], plane_peer[j])

    def dots_end(turn):
        arrived(all_dots.at[turn, pl.ds(0, NZH * NX - 1)], a_sem.at[turn])
        total = jnp.sum(all_dots[turn], axis=0)
        arrived(dof_dots.at[pl.ds(0, PARTS - 1)], d_send)
        arrived(pair_src, p_send)
        arrived(all_dots.at[turn, pl.ds(0, NZH * NX - 1)], a_send)
        return total[0:1] / (total[1:2] + 1e-06)

    def local_dots():
        im, res = image[...], res_ref[0]
        low, squares = column_sum(im * im), column_sum(res * res)
        dsrc[0:1] = column_sum(im * res)
        dsrc[1:2] = low
        dsrc[2:3] = squares
        return ratio(squares, low)

    def advance(alpha):
        sol_ref[0] = sol_ref[0] + alpha * v[...]
        res_ref[0] = res_ref[0] - alpha * image[...]

    begin_gather(rbuf, r_send, r_sem)
    for copy in loads_in[1:]:
        copy.wait()
    sp = jnp.broadcast_to(spring_row[...], (LOADS, ATT)).T
    spr[...] = sp
    main[...] = jnp.broadcast_to(diag_row[...], (LOADS, ROWS)).T
    main[:ATT] = main[:ATT] + sp
    sol_ref[0] = jnp.zeros((ROWS, LOADS), jnp.float32)
    dsrc[...] = jnp.zeros(dsrc.shape, jnp.float32)

    def first(idx):
        qold[idx] = pre_dot(idx)

    first(d)
    for event in range(COLUMN):
        first(take(rbuf, r_send, r_sem, event))
    for core in range(2):
        @pl.when(c == core)
        def _():
            for k in range(NY):
                for col in range(NZL):
                    at, to = (col * NY + k) * ATT + core * HALF, k * ATT + col * HALF
                    hubblk[:, to:to + HALF] = hubraw[:, at:at + HALF]
    take_across(rbuf, r_sem)
    for k in range(NY):
        first(across_first + k)
    total = qold[0]
    for k in range(1, PARTS):
        total = total + qold[k]
    vec[...] = total
    v[...] = total
    arrived(rbuf.at[pl.ds(0, BLOCKS)], r_send)
    apply_operator(0, lambda: None)
    image[...] = acc[...]

    def step(it, carry):
        turn = it % 2
        trial = local_dots()
        rbuf[d] = (res_ref[0] - trial * image[...]).astype(jnp.bfloat16)
        begin_gather(rbuf, r_send, r_sem)
        dots_begin()
        qnew[d] = pre_dot(d)
        for event in range(COLUMN):
            idx = take(rbuf, r_send, r_sem, event)
            qnew[idx] = pre_dot(idx)
            if event == 4:
                dots_pair()
        dots_plane(turn)

        def slope(idx, product):
            diff = (product - qold[idx]) / ratio(dof_dots[idx, 2:3], dof_dots[idx, 1:2])
            qnew[idx] = diff
            return diff

        total = jnp.zeros((ROWS, LOADS), jnp.float32)
        for k in range(NY):
            total = total + slope(zl * NY + k, qnew[zl * NY + k])
        take_across(rbuf, r_sem)
        for k in range(NY):
            total = total + slope(across_first + k, pre_dot(across_first + k))
        arrived(rbuf.at[pl.ds(0, BLOCKS)], r_send)
        alpha = dots_end(turn)
        vec[...] = v[...] + alpha * total

        def late():
            advance(alpha)
            v[...] = vec[...]
            for k in range(PARTS):
                qold[k] = qold[k] + alpha * qnew[k]

        apply_operator((it + 1) % 2, late)
        image[...] = acc[...]
        return carry

    lax.fori_loop(0, ITERS - 1, step, 0)
    last = (ITERS - 1) % 2
    local_dots()
    dots_begin()
    dots_pair()
    dots_plane(last)
    advance(dots_end(last))


def body(rhs, diagonal, coupling, springs, precond, hub_inverse):
    vm = pl.BlockSpec(memory_space=pltpu.VMEM)
    hbm = pl.BlockSpec(memory_space=pltpu.HBM)
    f32, bf16 = jnp.float32, jnp.bfloat16
    dma = pltpu.SemaphoreType.DMA
    mem = pltpu.VMEM
    return pl.pallas_call(
        kernel,
        out_shape=(
            jax.ShapeDtypeStruct((1, ROWS, LOADS), f32),
            jax.ShapeDtypeStruct((1, ROWS, LOADS), f32),
        ),
        in_specs=[hbm] * 6,
        out_specs=(vm, vm),
        scratch_shapes=[
            mem((1, ROWS), f32),
            mem((1, ATT), f32),
            mem((ROWS, PARTS * ROWS), bf16),
            mem((ROWS, PARTS * FACE), bf16),
            mem((ATT, PARTS * ATT), bf16),
            mem((ATT, NY * ATT), bf16),
            mem((PARTS, ROWS, LOADS), bf16),
            mem((2, PARTS, FACE, LOADS), bf16),
            mem((NY, NZL, HALF, LOADS), bf16),
            mem((PARTS, ROWS, LOADS), f32),
            mem((PARTS, ROWS, LOADS), f32),
            mem((FACE, LOADS), bf16),
            mem((ROWS, LOADS), f32),
            mem((ROWS, LOADS), f32),
            mem((ROWS, LOADS), f32),
            mem((ROWS, LOADS), f32),
            mem((ROWS, LOADS), f32),
            mem((ATT, LOADS), f32),
            mem((ATT, LOADS), f32),
            mem((ROWS, LOADS), f32),
            mem((ATT, LOADS), f32),
            mem((HALF, LOADS), f32),
            mem((HALF, LOADS), f32),
            mem((HALF, LOADS), f32),
            mem((2, NX, HALF, LOADS), f32),
            mem((HALF, LOADS), bf16),
            mem((2, NZ, HALF, LOADS), bf16),
            mem((8, LOADS), f32),
            mem((PARTS, 8, LOADS), f32),
            mem((8, LOADS), f32),
            mem((8, LOADS), f32),
            mem((2, NZH * NX, 8, LOADS), f32),
            dma((6,)),
            dma, dma((COLUMN + 1,)),
            dma, dma((COLUMN + 1,)),
            dma, dma((2, 2)),
            dma, dma,
            dma, dma((2,)),
            dma, dma((2,)),
            dma, dma,
            dma, dma,
            dma, dma,
            dma, dma,
            dma, dma((2,)),
        ],
        compiler_params=pltpu.CompilerParams(
            collective_id=0, has_side_effects=True, vmem_limit_bytes=63 * 1024 * 1024
        ),
    )(rhs, diagonal, springs, coupling, precond, hub_inverse)


def solution(mesh):
    placed = (
        P("sector", "dof", None),
        P("sector", "dof"),
        P("sector", "dof", None),
        P("sector", "dof"),
        P("dof", None),
        P("dof", None),
    )
    return jax.shard_map(
        body,
        mesh=mesh,
        in_specs=placed,
        out_specs=(P("sector", "dof", None), P("sector", "dof", None)),
        check_vma=False,
    )
```

time: 184 us -> 181 us (0.984)
  local copies, waits for them, and re-layouts: 7.65 us -> 3.14 us
  Pallas kernels: 175 us -> 177 us
    unnamed x14 -> x2, local copies, waits for them, and re-layouts: 7.65 us -> 3.14 us
    pallas_call x1, Pallas kernels: 175 us -> 177 us  [body(): pl.pallas_call(kernel, out_shape=(jax.ShapeDtypeStruct((1, ROWS, LOADS),...]
where the time goes in v3:
time: 181 us
  Pallas kernels  177 us (98%)
  local copies, waits for them, and re-layouts  3.14 us (2%)
    pallas_call x1, Pallas kernels, body(): pl.pallas_call(kernel, out_shape=(jax.ShapeDtypeStruct((1, ROWS, LOADS),...  177 us

profile of v3, /device:TPU:1, one launch (start us, length us, event | category | flops | bytes accessed | tf_op | source)
XLA Modules:
  0.0 181.2 jit_solution(989416617066558313)
XLA Ops:
  0.6 177.4 %shard_map.77 = (f32[1,256,128]{2,1,0:T(8,128)}, f32[1,256,128]{2,1,0:T(8,128)}) custom-call(f32[1,256,128]{2,1,0:T(8,128)} %rhs_hbm.1, f32[1,256]{1,0:T(1,128)} %diag_hbm.1, f32[1,192]{1,0:T(1,128)} %spring_hbm.1, bf16[1,256,2048]{2,1,0:T(8,128)(2,1)} %couple_hbm.1, bf16[256,4096]{1,0:T(8,128)(2,1)} %pre_hbm.1, bf16[192,3072]{1,0:T(8,128)(2,1)} %hub_hbm.1), custom_call_target="tpu_custom_call" | custom-call | tf_op jit(solution)/shard_map/pallas_call | solution.py:301
  178.1 1.6 copy.10
  179.6 1.6 copy.11

commit v4 on v3

--- a/solution.py
+++ b/solution.py
@@ -7,7 +7,6 @@
 
 ITERS = 3
 NX, NY, NZL, NZH = 4, 8, 2, 4
-NZ = NZL * NZH
 PARTS = NY * NZL
 QUARTER = 64
 ROWS = 4 * QUARTER
@@ -25,7 +24,7 @@
 def kernel(
     rhs_hbm, diag_hbm, spring_hbm, couple_hbm, pre_hbm, hub_hbm, sol_ref, res_ref,
     diag_row, spring_row, pre, coup, hubraw, hubblk, rbuf, fbuf, lbuf, qold, qnew, stage,
-    v, vec, image, acc, cacc, hacc, hrecv, main, spr, csend, crecv, xsend, xrecv, zsend, zrecv, dsrc, dof_dots, pair_src, pair_dots, all_dots,
+    v, vec, slopes, image, acc, cacc, hacc, hrecv, load, main, spr, csend, crecv, xsend, xrecv, zsend, zrecv, dsrc, dof_dots, pair_src, pair_dots, all_dots,
     load_sem, r_send, r_sem, f_send, f_sem, n_send, n_sem, c_send, c_sem, x_send, x_sem,
     z_send, z_sem, y_send, y_sem, h_send, h_sem, d_send, d_sem, p_send, p_sem, a_send, a_sem,
 ):
@@ -33,7 +32,6 @@
     d = lax.axis_index("dof")
     zh, x, c = s // (2 * NX), (s // 2) % NX, s % 2
     zl, y = d // NY, d % NY
-    z = zh * NZL + zl
     plane = zh * NX + x
     nsec = NZH * NX * 2
 
@@ -44,9 +42,7 @@
         col = zl if column == 0 else 1 - zl
         return col * NY + (y + offset + NY) % NY
 
-    y_peer = [(s, zl * NY + (y + j) % NY) for j in range(NY)]
-    z_at = [(z + j) % NZ for j in range(NZ)]
-    z_peer = [(sector_of(zz // NZL, x, c), (zz % NZL) * NY + y) for zz in z_at]
+    zh_peer = [(sector_of((zh + k) % NZH, x, c), d) for k in range(NZH)]
     x_peer = [(sector_of(zh, (x + j) % NX, c), d) for j in range(NX)]
     dof_peer = [(s, (d + j) % PARTS) for j in range(PARTS)]
     plane_at = [(plane + j) % (NZH * NX) for j in range(NZH * NX)]
@@ -73,14 +69,12 @@
         pltpu.make_async_copy(hub_hbm, hubraw, load_sem.at[4]),
         pltpu.make_async_copy(couple_hbm.at[0], coup, load_sem.at[5]),
     ]
+    barrier = pltpu.get_barrier_semaphore()
+    greet = plane_peer[1:] + dof_peer[1:] + [sibling, next_sec, prev_sec]
+    for dev in greet:
+        pl.semaphore_signal(barrier, inc=1, device_id=dev, device_id_type=MESH)
     for copy in loads_in:
         copy.start()
-
-    barrier = pltpu.get_barrier_semaphore()
-    greet = dof_peer[1:] + plane_peer[1:] + z_peer[1::2] + [sibling, next_sec, prev_sec]
-    for dev in greet:
-        pl.semaphore_signal(barrier, inc=1, device_id=dev, device_id_type=MESH)
-
     loads_in[0].wait()
     rbuf[d] = res_ref[0].astype(jnp.bfloat16)
     pl.semaphore_wait(barrier, len(greet))
@@ -113,61 +107,58 @@
     def ratio(squares, low):
         return jnp.clip(jnp.sqrt(squares / jnp.maximum(low, 1e-30)), 1e-12, 1e12)
 
-    def apply_operator(turn, late):
+    def apply_operator(turn, source, settle, late):
         faces = fbuf.at[turn]
         other = pl.multiple_of((1 - c) * HALF, 8)
         mine = pl.multiple_of(c * HALF, 8)
-        csend[...] = spr[pl.ds(other, HALF)] * vec[pl.ds(other, HALF)]
+        csend[...] = spr[pl.ds(other, HALF)] * source[pl.ds(other, HALF)]
         send(csend, crecv, c_send, c_sem, sibling)
-        stage[...] = vec[:FACE].astype(jnp.bfloat16)
-        right, left = pl.ds(QUARTER, QUARTER), pl.ds(0, QUARTER)
-        send(stage.at[right], faces.at[d, left], n_send, n_sem.at[turn, 0], next_sec)
-        send(stage.at[left], faces.at[d, right], n_send, n_sem.at[turn, 1], prev_sec)
-        part = spr[pl.ds(mine, HALF)] * vec[pl.ds(mine, HALF)]
+        part = spr[pl.ds(mine, HALF)] * source[pl.ds(mine, HALF)]
         arrived(crecv, c_sem)
         part = part + crecv[...]
         xsend[...] = part
         for j in range(1, NX):
             send(xsend, xrecv.at[turn, j], x_send, x_sem.at[turn], x_peer[j])
+        arrived(xrecv.at[turn, pl.ds(1, NX - 1)], x_sem.at[turn])
+        part = part + xrecv[turn, 1] + xrecv[turn, 2] + xrecv[turn, 3]
+        zsend[...] = part
+        for k in range(1, NZH):
+            send(zsend, zrecv.at[turn, k], z_send, z_sem.at[turn], zh_peer[k])
+        alpha = settle()
+        stage[...] = vec[:FACE].astype(jnp.bfloat16)
+        right, left = pl.ds(QUARTER, QUARTER), pl.ds(0, QUARTER)
+        send(stage.at[right], faces.at[d, left], n_send, n_sem.at[turn, 0], next_sec)
+        send(stage.at[left], faces.at[d, right], n_send, n_sem.at[turn, 1], prev_sec)
+        late(alpha)
         arrived(faces.at[d, left], n_sem.at[turn, 0])
         arrived(faces.at[d, right], n_sem.at[turn, 1])
         begin_gather(faces, f_send, f_sem)
-        arrived(xrecv.at[turn, pl.ds(1, NX - 1)], x_sem.at[turn])
-        part = part + xrecv[turn, 1] + xrecv[turn, 2] + xrecv[turn, 3]
-        zsend[...] = part.astype(jnp.bfloat16)
-        for j in range(1, NZ):
-            send(zsend, zrecv.at[turn, j], z_send, z_sem.at[turn], z_peer[j])
         cacc[...] = couple_dot(faces, d, 1)
+        arrived(zrecv.at[turn, pl.ds(1, NZH - 1)], z_sem.at[turn])
+        part = part + zrecv[turn, 1] + zrecv[turn, 2] + zrecv[turn, 3]
+        part = load[...] + alpha * part
+        load[...] = part
+        lbuf[d] = part.astype(jnp.bfloat16)
+        begin_gather(lbuf, y_send, y_sem)
         for event in range(COLUMN):
             cacc[...] += couple_dot(faces, take(faces, f_send, f_sem, event), 1)
-        arrived(zrecv.at[turn, pl.ds(1, NZ - 1)], z_sem.at[turn])
-        across = zrecv[turn, 1].astype(jnp.float32)
-        for j in range(2, NZ):
-            term = zrecv[turn, j].astype(jnp.float32)
-            if j % 2 == 0:
-                part = part + term
-            else:
-                across = across + term
-        lbuf[y, zl] = part.astype(jnp.bfloat16)
-        lbuf[y, 1 - zl] = across.astype(jnp.bfloat16)
-        for j in range(1, NY):
-            send(lbuf.at[y], lbuf.at[y], y_send, y_sem, y_peer[j])
+        for event in range(COLUMN):
+            take(lbuf, y_send, y_sem, event)
         take_across(faces, f_sem)
         acc[...] = main[...] * vec[...] + cacc[...] + couple_dot(faces, across_first, NY)
-        late()
         arrived(csend, c_send)
         arrived(stage, n_send)
         arrived(xrecv.at[turn, pl.ds(0, NX - 1)], x_send)
         arrived(faces.at[pl.ds(0, BLOCKS)], f_send)
-        arrived(zrecv.at[turn, pl.ds(0, NZ - 1)], z_send)
-        arrived(lbuf.at[pl.ds(0, NY - 1)], y_send)
-        arrived(lbuf.at[pl.ds(0, NY - 1)], y_sem)
-        rows = lbuf[...].reshape(NY * ATT, LOADS)
+        arrived(zrecv.at[turn, pl.ds(0, NZH - 1)], z_send)
+        take_across(lbuf, y_sem)
+        rows = lbuf[...].reshape(PARTS * HALF, LOADS)
         hacc[...] = jnp.dot(hubblk[...], rows, preferred_element_type=jnp.float32)
         send(hacc, hrecv, h_send, h_sem, sibling)
         arrived(hrecv, h_sem)
         acc[:ATT] = acc[:ATT] - spr[...] * (hacc[...] + hrecv[...])
         arrived(hacc, h_send)
+        arrived(lbuf.at[pl.ds(0, BLOCKS)], y_send)
 
     def column_sum(a):
         return jnp.sum(a, axis=0, keepdims=True)
@@ -228,10 +219,9 @@
     for core in range(2):
         @pl.when(c == core)
         def _():
-            for k in range(NY):
-                for col in range(NZL):
-                    at, to = (col * NY + k) * ATT + core * HALF, k * ATT + col * HALF
-                    hubblk[:, to:to + HALF] = hubraw[:, at:at + HALF]
+            for k in range(PARTS):
+                at, to = k * ATT + core * HALF, k * HALF
+                hubblk[:, to:to + HALF] = hubraw[:, at:at + HALF]
     take_across(rbuf, r_sem)
     for k in range(NY):
         first(across_first + k)
@@ -241,22 +231,24 @@
     vec[...] = total
     v[...] = total
     arrived(rbuf.at[pl.ds(0, BLOCKS)], r_send)
-    apply_operator(0, lambda: None)
+    load[...] = jnp.zeros((HALF, LOADS), jnp.float32)
+    apply_operator(0, vec, lambda: 1.0, lambda alpha: None)
     image[...] = acc[...]
 
     def step(it, carry):
         turn = it % 2
         trial = local_dots()
+        dots_begin()
         rbuf[d] = (res_ref[0] - trial * image[...]).astype(jnp.bfloat16)
         begin_gather(rbuf, r_send, r_sem)
-        dots_begin()
         qnew[d] = pre_dot(d)
         for event in range(COLUMN):
             idx = take(rbuf, r_send, r_sem, event)
             qnew[idx] = pre_dot(idx)
-            if event == 4:
+            if event == 3:
                 dots_pair()
-        dots_plane(turn)
+            if event == 5:
+                dots_plane(turn)
 
         def slope(idx, product):
             diff = (product - qold[idx]) / ratio(dof_dots[idx, 2:3], dof_dots[idx, 1:2])
@@ -270,16 +262,20 @@
         for k in range(NY):
             total = total + slope(across_first + k, pre_dot(across_first + k))
         arrived(rbuf.at[pl.ds(0, BLOCKS)], r_send)
-        alpha = dots_end(turn)
-        vec[...] = v[...] + alpha * total
-
-        def late():
+        slopes[...] = total
+
+        def settle():
+            alpha = dots_end(turn)
+            vec[...] = v[...] + alpha * slopes[...]
+            return alpha
+
+        def late(alpha):
             advance(alpha)
             v[...] = vec[...]
             for k in range(PARTS):
                 qold[k] = qold[k] + alpha * qnew[k]
 
-        apply_operator((it + 1) % 2, late)
+        apply_operator((it + 1) % 2, slopes, settle, late)
         image[...] = acc[...]
         return carry
 
@@ -312,10 +308,10 @@
             mem((ROWS, PARTS * ROWS), bf16),
             mem((ROWS, PARTS * FACE), bf16),
             mem((ATT, PARTS * ATT), bf16),
-            mem((ATT, NY * ATT), bf16),
+            mem((ATT, PARTS * HALF), bf16),
             mem((PARTS, ROWS, LOADS), bf16),
             mem((2, PARTS, FACE, LOADS), bf16),
-            mem((NY, NZL, HALF, LOADS), bf16),
+            mem((PARTS, HALF, LOADS), bf16),
             mem((PARTS, ROWS, LOADS), f32),
             mem((PARTS, ROWS, LOADS), f32),
             mem((FACE, LOADS), bf16),
@@ -324,16 +320,18 @@
             mem((ROWS, LOADS), f32),
             mem((ROWS, LOADS), f32),
             mem((ROWS, LOADS), f32),
+            mem((ROWS, LOADS), f32),
             mem((ATT, LOADS), f32),
             mem((ATT, LOADS), f32),
+            mem((HALF, LOADS), f32),
             mem((ROWS, LOADS), f32),
             mem((ATT, LOADS), f32),
             mem((HALF, LOADS), f32),
             mem((HALF, LOADS), f32),
             mem((HALF, LOADS), f32),
             mem((2, NX, HALF, LOADS), f32),
-            mem((HALF, LOADS), bf16),
-            mem((2, NZ, HALF, LOADS), bf16),
+            mem((HALF, LOADS), f32),
+            mem((2, NZH, HALF, LOADS), f32),
             mem((8, LOADS), f32),
             mem((PARTS, 8, LOADS), f32),
             mem((8, LOADS), f32),
@@ -346,14 +344,14 @@
             dma, dma,
             dma, dma((2,)),
             dma, dma((2,)),
-            dma, dma,
+            dma, dma((COLUMN + 1,)),
             dma, dma,
             dma, dma,
             dma, dma,
             dma, dma((2,)),
         ],
         compiler_params=pltpu.CompilerParams(
-            collective_id=0, has_side_effects=True, vmem_limit_bytes=63 * 1024 * 1024
+            collective_id=0, has_side_effects=True, vmem_limit_bytes=61 * 1024 * 1024
         ),
     )(rhs, diagonal, springs, coupling, precond, hub_inverse)
 

time: 181 us -> 174 us (0.961)
  Pallas kernels: 177 us -> 170 us
    pallas_call x1, Pallas kernels: 177 us -> 170 us  [body(): pl.pallas_call(kernel, out_shape=(jax.ShapeDtypeStruct((1, ROWS, LOADS),...]
where the time goes in v4:
time: 174 us
  Pallas kernels  170 us (98%)
  local copies, waits for them, and re-layouts  3.14 us (2%)
    pallas_call x1, Pallas kernels, body(): pl.pallas_call(kernel, out_shape=(jax.ShapeDtypeStruct((1, ROWS, LOADS),...  170 us

profile of v4, /device:TPU:1, one launch (start us, length us, event | category | flops | bytes accessed | tf_op | source)
XLA Modules:
  0.0 174.2 jit_solution(1104126021965388697)
XLA Ops:
  0.6 170.4 %shard_map.77 = (f32[1,256,128]{2,1,0:T(8,128)}, f32[1,256,128]{2,1,0:T(8,128)}) custom-call(f32[1,256,128]{2,1,0:T(8,128)} %rhs_hbm.1, f32[1,256]{1,0:T(1,128)} %diag_hbm.1, f32[1,192]{1,0:T(1,128)} %spring_hbm.1, bf16[1,256,2048]{2,1,0:T(8,128)(2,1)} %couple_hbm.1, bf16[256,4096]{1,0:T(8,128)(2,1)} %pre_hbm.1, bf16[192,3072]{1,0:T(8,128)(2,1)} %hub_hbm.1), custom_call_target="tpu_custom_call" | custom-call | tf_op jit(solution)/shard_map/pallas_call | solution.py:297
  171.1 1.6 copy.10
  172.6 1.6 copy.11

commit v5 on v4

--- a/solution.py
+++ b/solution.py
@@ -24,7 +24,7 @@
 def kernel(
     rhs_hbm, diag_hbm, spring_hbm, couple_hbm, pre_hbm, hub_hbm, sol_ref, res_ref,
     diag_row, spring_row, pre, coup, hubraw, hubblk, rbuf, fbuf, lbuf, qold, qnew, stage,
-    v, vec, slopes, image, acc, cacc, hacc, hrecv, load, main, spr, csend, crecv, xsend, xrecv, zsend, zrecv, dsrc, dof_dots, pair_src, pair_dots, all_dots,
+    v, vec, slopes, inverse, image, acc, cacc, hacc, hrecv, load, main, spr, csend, crecv, xsend, xrecv, zsend, zrecv, dsrc, dof_dots, pair_src, pair_dots, all_dots,
     load_sem, r_send, r_sem, f_send, f_sem, n_send, n_sem, c_send, c_sem, x_send, x_sem,
     z_send, z_sem, y_send, y_sem, h_send, h_sem, d_send, d_sem, p_send, p_sem, a_send, a_sem,
 ):
@@ -84,10 +84,15 @@
             send(buf.at[d], buf.at[d], ssem, rsem.at[k], (s, dof_at(0, -offset)))
         send(buf.at[d], buf.at[d], ssem, rsem.at[COLUMN], partner)
 
-    def take(buf, ssem, rsem, event):
+    def take(buf, ssem, rsem, event, onward=COLUMN):
         idx = dof_at(0, NEAR[event])
         arrived(buf.at[idx], rsem.at[event])
-        send(buf.at[idx], buf.at[idx], ssem, rsem.at[COLUMN], partner)
+        send(buf.at[idx], buf.at[idx], ssem, rsem.at[onward], partner)
+        return idx
+
+    def take_one_across(event):
+        idx = dof_at(1, ((0,) + NEAR)[event])
+        arrived(rbuf.at[idx], r_sem.at[COLUMN + event])
         return idx
 
     across_first = (1 - zl) * NY
@@ -109,41 +114,65 @@
 
     def apply_operator(turn, source, settle, late):
         faces = fbuf.at[turn]
+        right, left = pl.ds(QUARTER, QUARTER), pl.ds(0, QUARTER)
+
+        def send_faces():
+            stage[...] = vec[:FACE].astype(jnp.bfloat16)
+            send(stage.at[right], faces.at[d, left], n_send, n_sem.at[turn, 0], next_sec)
+            send(stage.at[left], faces.at[d, right], n_send, n_sem.at[turn, 1], prev_sec)
+
+        def gather_faces():
+            arrived(faces.at[d, left], n_sem.at[turn, 0])
+            arrived(faces.at[d, right], n_sem.at[turn, 1])
+            begin_gather(faces, f_send, f_sem)
+
+        def face(event):
+            cacc[...] += couple_dot(faces, take(faces, f_send, f_sem, event), 1)
+
         other = pl.multiple_of((1 - c) * HALF, 8)
         mine = pl.multiple_of(c * HALF, 8)
         csend[...] = spr[pl.ds(other, HALF)] * source[pl.ds(other, HALF)]
         send(csend, crecv, c_send, c_sem, sibling)
+        if settle is None:
+            send_faces()
         part = spr[pl.ds(mine, HALF)] * source[pl.ds(mine, HALF)]
         arrived(crecv, c_sem)
         part = part + crecv[...]
         xsend[...] = part
         for j in range(1, NX):
             send(xsend, xrecv.at[turn, j], x_send, x_sem.at[turn], x_peer[j])
+        if settle is None:
+            gather_faces()
         arrived(xrecv.at[turn, pl.ds(1, NX - 1)], x_sem.at[turn])
         part = part + xrecv[turn, 1] + xrecv[turn, 2] + xrecv[turn, 3]
         zsend[...] = part
         for k in range(1, NZH):
             send(zsend, zrecv.at[turn, k], z_send, z_sem.at[turn], zh_peer[k])
-        alpha = settle()
-        stage[...] = vec[:FACE].astype(jnp.bfloat16)
-        right, left = pl.ds(QUARTER, QUARTER), pl.ds(0, QUARTER)
-        send(stage.at[right], faces.at[d, left], n_send, n_sem.at[turn, 0], next_sec)
-        send(stage.at[left], faces.at[d, right], n_send, n_sem.at[turn, 1], prev_sec)
-        late(alpha)
-        arrived(faces.at[d, left], n_sem.at[turn, 0])
-        arrived(faces.at[d, right], n_sem.at[turn, 1])
-        begin_gather(faces, f_send, f_sem)
-        cacc[...] = couple_dot(faces, d, 1)
+        ahead = 0
+        if settle is None:
+            cacc[...] = couple_dot(faces, d, 1)
+            for event in range(COLUMN):
+                face(event)
+            ahead = COLUMN
+        else:
+            alpha = settle()
+            send_faces()
+            late(alpha)
+            gather_faces()
+            cacc[...] = couple_dot(faces, d, 1)
         arrived(zrecv.at[turn, pl.ds(1, NZH - 1)], z_sem.at[turn])
         part = part + zrecv[turn, 1] + zrecv[turn, 2] + zrecv[turn, 3]
-        part = load[...] + alpha * part
+        if settle is not None:
+            part = load[...] + alpha * part
         load[...] = part
         lbuf[d] = part.astype(jnp.bfloat16)
         begin_gather(lbuf, y_send, y_sem)
-        for event in range(COLUMN):
-            cacc[...] += couple_dot(faces, take(faces, f_send, f_sem, event), 1)
+        for event in range(ahead, 4):
+            face(event)
         for event in range(COLUMN):
             take(lbuf, y_send, y_sem, event)
+            if max(ahead, 4) <= event + 4 < COLUMN:
+                face(event + 4)
         take_across(faces, f_sem)
         acc[...] = main[...] * vec[...] + cacc[...] + couple_dot(faces, across_first, NY)
         arrived(csend, c_send)
@@ -215,54 +244,55 @@
 
     first(d)
     for event in range(COLUMN):
-        first(take(rbuf, r_send, r_sem, event))
+        first(take(rbuf, r_send, r_sem, event, COLUMN + 1 + event))
     for core in range(2):
         @pl.when(c == core)
         def _():
             for k in range(PARTS):
                 at, to = k * ATT + core * HALF, k * HALF
                 hubblk[:, to:to + HALF] = hubraw[:, at:at + HALF]
-    take_across(rbuf, r_sem)
-    for k in range(NY):
-        first(across_first + k)
-    total = qold[0]
-    for k in range(1, PARTS):
-        total = total + qold[k]
+    total = qold[zl * NY]
+    for k in range(1, NY):
+        total = total + qold[zl * NY + k]
     vec[...] = total
-    v[...] = total
+    for event in range(NY):
+        idx = take_one_across(event)
+        product = pre_dot(idx)
+        qold[idx] = product
+        vec[...] += product
+    v[...] = vec[...]
     arrived(rbuf.at[pl.ds(0, BLOCKS)], r_send)
-    load[...] = jnp.zeros((HALF, LOADS), jnp.float32)
-    apply_operator(0, vec, lambda: 1.0, lambda alpha: None)
+    apply_operator(0, vec, None, None)
     image[...] = acc[...]
 
     def step(it, carry):
         turn = it % 2
         trial = local_dots()
-        dots_begin()
         rbuf[d] = (res_ref[0] - trial * image[...]).astype(jnp.bfloat16)
         begin_gather(rbuf, r_send, r_sem)
+        dots_begin()
         qnew[d] = pre_dot(d)
         for event in range(COLUMN):
-            idx = take(rbuf, r_send, r_sem, event)
+            idx = take(rbuf, r_send, r_sem, event, COLUMN + 1 + event)
             qnew[idx] = pre_dot(idx)
-            if event == 3:
+            if event == 4:
                 dots_pair()
-            if event == 5:
-                dots_plane(turn)
+        dots_plane(turn)
+        inverse[...] = 1.0 / ratio(dof_dots[:, 2, :], dof_dots[:, 1, :])
 
         def slope(idx, product):
-            diff = (product - qold[idx]) / ratio(dof_dots[idx, 2:3], dof_dots[idx, 1:2])
+            diff = (product - qold[idx]) * inverse[pl.ds(idx, 1)]
             qnew[idx] = diff
             return diff
 
         total = jnp.zeros((ROWS, LOADS), jnp.float32)
         for k in range(NY):
             total = total + slope(zl * NY + k, qnew[zl * NY + k])
-        take_across(rbuf, r_sem)
-        for k in range(NY):
-            total = total + slope(across_first + k, pre_dot(across_first + k))
+        slopes[...] = total
+        for event in range(NY):
+            idx = take_one_across(event)
+            slopes[...] += slope(idx, pre_dot(idx))
         arrived(rbuf.at[pl.ds(0, BLOCKS)], r_send)
-        slopes[...] = total
 
         def settle():
             alpha = dots_end(turn)
@@ -318,6 +348,7 @@
             mem((ROWS, LOADS), f32),
             mem((ROWS, LOADS), f32),
             mem((ROWS, LOADS), f32),
+            mem((PARTS, LOADS), f32),
             mem((ROWS, LOADS), f32),
             mem((ROWS, LOADS), f32),
             mem((ROWS, LOADS), f32),
@@ -338,7 +369,7 @@
             mem((8, LOADS), f32),
             mem((2, NZH * NX, 8, LOADS), f32),
             dma((6,)),
-            dma, dma((COLUMN + 1,)),
+            dma, dma((BLOCKS,)),
             dma, dma((COLUMN + 1,)),
             dma, dma((2, 2)),
             dma, dma,

time: 174 us -> 173 us (level)
  no operation moved by 1% of the time
where the time goes in v5:
time: 173 us
  Pallas kernels  169 us (98%)
  local copies, waits for them, and re-layouts  3.14 us (2%)
    pallas_call x1, Pallas kernels, body(): pl.pallas_call(kernel, out_shape=(jax.ShapeDtypeStruct((1, ROWS, LOADS),...  169 us

profile of v5, /device:TPU:1, one launch (start us, length us, event | category | flops | bytes accessed | tf_op | source)
XLA Modules:
  0.0 173.1 jit_solution(12834068676858334604)
XLA Ops:
  0.6 169.4 %shard_map.77 = (f32[1,256,128]{2,1,0:T(8,128)}, f32[1,256,128]{2,1,0:T(8,128)}) custom-call(f32[1,256,128]{2,1,0:T(8,128)} %rhs_hbm.1, f32[1,256]{1,0:T(1,128)} %diag_hbm.1, f32[1,192]{1,0:T(1,128)} %spring_hbm.1, bf16[1,256,2048]{2,1,0:T(8,128)(2,1)} %couple_hbm.1, bf16[256,4096]{1,0:T(8,128)(2,1)} %pre_hbm.1, bf16[192,3072]{1,0:T(8,128)(2,1)} %hub_hbm.1), custom_call_target="tpu_custom_call" | custom-call | tf_op jit(solution)/shard_map/pallas_call | solution.py:327
  170.0 1.6 copy.10
  171.6 1.6 copy.11

commit v6 on v5

--- a/solution.py
+++ b/solution.py
@@ -16,7 +16,7 @@
 LOADS = 128
 MESH = pl.DeviceIdType.MESH
 
-NEAR = (-1, 1, -2, 2, -3, 3, 4)
+NEAR = (-2, 2, -1, 1, -3, 3, -4)
 COLUMN = len(NEAR)
 BLOCKS = 2 * COLUMN + 1
 
@@ -80,13 +80,15 @@
     pl.semaphore_wait(barrier, len(greet))
 
     def begin_gather(buf, ssem, rsem):
-        for k, offset in enumerate(NEAR):
+        for k, offset in enumerate(NEAR[:-1]):
             send(buf.at[d], buf.at[d], ssem, rsem.at[k], (s, dof_at(0, -offset)))
         send(buf.at[d], buf.at[d], ssem, rsem.at[COLUMN], partner)
 
     def take(buf, ssem, rsem, event, onward=COLUMN):
         idx = dof_at(0, NEAR[event])
         arrived(buf.at[idx], rsem.at[event])
+        if event == 0:
+            send(buf.at[idx], buf.at[idx], ssem, rsem.at[COLUMN - 1], (s, dof_at(0, 2)))
         send(buf.at[idx], buf.at[idx], ssem, rsem.at[onward], partner)
         return idx
 

time: 173 us -> 171 us (0.988)
  Pallas kernels: 169 us -> 167 us
    pallas_call x1, Pallas kernels: 169 us -> 167 us  [body(): pl.pallas_call(kernel, out_shape=(jax.ShapeDtypeStruct((1, ROWS, LOADS),...]
where the time goes in v6:
time: 171 us; the launch traced here: 170 us
  Pallas kernels  167 us (98%)
  local copies, waits for them, and re-layouts  3.14 us (2%)
    pallas_call x1, Pallas kernels, body(): pl.pallas_call(kernel, out_shape=(jax.ShapeDtypeStruct((1, ROWS, LOADS),...  167 us

profile of v6, /device:TPU:1, one launch (start us, length us, event | category | flops | bytes accessed | tf_op | source)
XLA Modules:
  0.0 170.4 jit_solution(9329254915734621099)
XLA Ops:
  0.6 166.7 %shard_map.77 = (f32[1,256,128]{2,1,0:T(8,128)}, f32[1,256,128]{2,1,0:T(8,128)}) custom-call(f32[1,256,128]{2,1,0:T(8,128)} %rhs_hbm.1, f32[1,256]{1,0:T(1,128)} %diag_hbm.1, f32[1,192]{1,0:T(1,128)} %spring_hbm.1, bf16[1,256,2048]{2,1,0:T(8,128)(2,1)} %couple_hbm.1, bf16[256,4096]{1,0:T(8,128)(2,1)} %pre_hbm.1, bf16[192,3072]{1,0:T(8,128)(2,1)} %hub_hbm.1), custom_call_target="tpu_custom_call" | custom-call | tf_op jit(solution)/shard_map/pallas_call | solution.py:329
  167.3 1.6 copy.10
  168.9 1.6 copy.11

commit v7 on v6

--- a/solution.py
+++ b/solution.py
@@ -22,9 +22,9 @@
 
 
 def kernel(
-    rhs_hbm, diag_hbm, spring_hbm, couple_hbm, pre_hbm, hub_hbm, sol_ref, res_ref,
+    rhs_hbm, diag_hbm, spring_hbm, couple_hbm, pre_hbm, hub_hbm, sol_ref, res_ref, v, image,
     diag_row, spring_row, pre, coup, hubraw, hubblk, rbuf, fbuf, lbuf, qold, qnew, stage,
-    v, vec, slopes, inverse, image, acc, cacc, hacc, hrecv, load, main, spr, csend, crecv, xsend, xrecv, zsend, zrecv, dsrc, dof_dots, pair_src, pair_dots, all_dots,
+    vec, slopes, inverse, acc, cacc, hacc, hrecv, load, main, spr, csend, crecv, xsend, xrecv, zsend, zrecv, dsrc, dof_dots, pair_src, pair_dots, all_dots,
     load_sem, r_send, r_sem, f_send, f_sem, n_send, n_sem, c_send, c_sem, x_send, x_sem,
     z_send, z_sem, y_send, y_sem, h_send, h_sem, d_send, d_sem, p_send, p_sem, a_send, a_sem,
 ):
@@ -145,6 +145,10 @@
             send(xsend, xrecv.at[turn, j], x_send, x_sem.at[turn], x_peer[j])
         if settle is None:
             gather_faces()
+        else:
+            alpha = settle()
+            send_faces()
+            late(alpha)
         arrived(xrecv.at[turn, pl.ds(1, NX - 1)], x_sem.at[turn])
         part = part + xrecv[turn, 1] + xrecv[turn, 2] + xrecv[turn, 3]
         zsend[...] = part
@@ -157,9 +161,6 @@
                 face(event)
             ahead = COLUMN
         else:
-            alpha = settle()
-            send_faces()
-            late(alpha)
             gather_faces()
             cacc[...] = couple_dot(faces, d, 1)
         arrived(zrecv.at[turn, pl.ds(1, NZH - 1)], z_sem.at[turn])
@@ -195,6 +196,7 @@
         return jnp.sum(a, axis=0, keepdims=True)
 
     def dots_begin():
+        dsrc[0:1] = column_sum(image[...] * res_ref[0])
         for j in range(1, PARTS):
             send(dsrc, dof_dots.at[d], d_send, d_sem, dof_peer[j])
         dof_dots[d] = dsrc[...]
@@ -222,7 +224,6 @@
     def local_dots():
         im, res = image[...], res_ref[0]
         low, squares = column_sum(im * im), column_sum(res * res)
-        dsrc[0:1] = column_sum(im * res)
         dsrc[1:2] = low
         dsrc[2:3] = squares
         return ratio(squares, low)
@@ -317,7 +318,9 @@
     dots_begin()
     dots_pair()
     dots_plane(last)
-    advance(dots_end(last))
+    alpha = dots_end(last)
+    v[...] = alpha * v[...]
+    image[...] = alpha * image[...]
 
 
 def body(rhs, diagonal, coupling, springs, precond, hub_inverse):
@@ -326,14 +329,16 @@
     f32, bf16 = jnp.float32, jnp.bfloat16
     dma = pltpu.SemaphoreType.DMA
     mem = pltpu.VMEM
-    return pl.pallas_call(
+    total, res, v, image = pl.pallas_call(
         kernel,
         out_shape=(
             jax.ShapeDtypeStruct((1, ROWS, LOADS), f32),
             jax.ShapeDtypeStruct((1, ROWS, LOADS), f32),
+            jax.ShapeDtypeStruct((ROWS, LOADS), f32),
+            jax.ShapeDtypeStruct((ROWS, LOADS), f32),
         ),
         in_specs=[hbm] * 6,
-        out_specs=(vm, vm),
+        out_specs=(vm,) * 4,
         scratch_shapes=[
             mem((1, ROWS), f32),
             mem((1, ATT), f32),
@@ -349,9 +354,7 @@
             mem((FACE, LOADS), bf16),
             mem((ROWS, LOADS), f32),
             mem((ROWS, LOADS), f32),
-            mem((ROWS, LOADS), f32),
             mem((PARTS, LOADS), f32),
-            mem((ROWS, LOADS), f32),
             mem((ROWS, LOADS), f32),
             mem((ROWS, LOADS), f32),
             mem((ATT, LOADS), f32),
@@ -387,6 +390,7 @@
             collective_id=0, has_side_effects=True, vmem_limit_bytes=61 * 1024 * 1024
         ),
     )(rhs, diagonal, springs, coupling, precond, hub_inverse)
+    return total + v, res - image
 
 
 def solution(mesh):

time: 171 us -> 166 us (0.971)
  local copies, waits for them, and re-layouts: 3.14 us -> 0 us
  Pallas kernels: 167 us -> 164 us
  other arithmetic: 0 us -> 1.82 us
    unnamed x2 -> x0, local copies, waits for them, and re-layouts: 3.14 us -> none
    pallas_call x1, Pallas kernels: 167 us -> 164 us  [body(): pl.pallas_call(kernel, out_shape=(jax.ShapeDtypeStruct((1, ROWS, LOADS),...]
    sub x0 -> x1, other arithmetic: none -> 1.82 us  [body(): return (total + v, res - image)]
where the time goes in v7:
time: 166 us
  Pallas kernels  164 us (99%)
  other arithmetic  1.82 us (1%)
    pallas_call x1, Pallas kernels, body(): pl.pallas_call(kernel, out_shape=(jax.ShapeDtypeStruct((1, ROWS, LOADS),...  164 us

profile of v7, /device:TPU:1, one launch (start us, length us, event | category | flops | bytes accessed | tf_op | source)
XLA Modules:
  0.0 166.2 jit_solution(13941571473783629270)
XLA Ops:
  0.6 163.7 %shard_map.77 = (f32[1,256,128]{2,1,0:T(8,128)}, f32[1,256,128]{2,1,0:T(8,128)}, f32[256,128]{1,0:T(8,128)}, f32[256,128]{1,0:T(8,128)}) custom-call(f32[1,256,128]{2,1,0:T(8,128)} %rhs_hbm.1, f32[1,256]{1,0:T(1,128)} %diag_hbm.1, f32[1,192]{1,0:T(1,128)} %spring_hbm.1, bf16[1,256,2048]{2,1,0:T(8,128)(2,1)} %couple_hbm.1, bf16[256,4096]{1,0:T(8,128)(2,1)} %pre_hbm.1, ...), custom_call_target="tpu_custom_call" | custom-call | tf_op jit(solution)/shard_map/pallas_call | solution.py:332
  164.4 1.8 %bitcast_subtract_fusion = (f32[1,256,128]{2,1,0:T(8,128)}, f32[1,256,128]{2,1,0:T(8,128)}) fusion(f32[1,256,128]{2,1,0:T(8,128)} %get-tuple-element.8, f32[256,128]{1,0:T(8,128)} %get-tuple-element.9, f32[1,256,128]{2,1,0:T(8,128)} %get-tuple-element.6, f32[256,128]{1,0:T(8,128)} %get-tuple-element.7), kind=kLoop, calls=%fused_computation | loop fusion | flops 65536 | bytes 786432 | tf_op jit(solution)/shard_map/sub | solution.py:393

commit v8 on v7

--- a/solution.py
+++ b/solution.py
@@ -110,6 +110,11 @@
         off = pl.multiple_of(first * FACE, FACE)
         rows = faces[pl.ds(first, count)].reshape(count * FACE, LOADS)
         return jnp.dot(coup[:, pl.ds(off, count * FACE)], rows, preferred_element_type=jnp.float32)
+
+    def hub_dot(first):
+        off = pl.multiple_of(first * HALF, NY * HALF)
+        rows = lbuf[pl.ds(first, NY)].reshape(NY * HALF, LOADS)
+        return jnp.dot(hubblk[:, pl.ds(off, NY * HALF)], rows, preferred_element_type=jnp.float32)
 
     def ratio(squares, low):
         return jnp.clip(jnp.sqrt(squares / jnp.maximum(low, 1e-30)), 1e-12, 1e12)
@@ -183,9 +188,9 @@
         arrived(xrecv.at[turn, pl.ds(0, NX - 1)], x_send)
         arrived(faces.at[pl.ds(0, BLOCKS)], f_send)
         arrived(zrecv.at[turn, pl.ds(0, NZH - 1)], z_send)
+        hacc[...] = hub_dot(zl * NY)
         take_across(lbuf, y_sem)
-        rows = lbuf[...].reshape(PARTS * HALF, LOADS)
-        hacc[...] = jnp.dot(hubblk[...], rows, preferred_element_type=jnp.float32)
+        hacc[...] += hub_dot(across_first)
         send(hacc, hrecv, h_send, h_sem, sibling)
         arrived(hrecv, h_sem)
         acc[:ATT] = acc[:ATT] - spr[...] * (hacc[...] + hrecv[...])
@@ -278,9 +283,10 @@
         for event in range(COLUMN):
             idx = take(rbuf, r_send, r_sem, event, COLUMN + 1 + event)
             qnew[idx] = pre_dot(idx)
-            if event == 4:
+            if event == 3:
                 dots_pair()
-        dots_plane(turn)
+            if event == 5:
+                dots_plane(turn)
         inverse[...] = 1.0 / ratio(dof_dots[:, 2, :], dof_dots[:, 1, :])
 
         def slope(idx, product):

time: 166 us -> 170 us (1.024)
  Pallas kernels: 164 us -> 167 us
    pallas_call x1, Pallas kernels: 164 us -> 167 us  [body(): pl.pallas_call(kernel, out_shape=(jax.ShapeDtypeStruct((1, ROWS, LOADS),...]
where the time goes in v8:
time: 170 us; the launch traced here: 169 us
  Pallas kernels  167 us (98%)
  other arithmetic  1.82 us (1%)
    pallas_call x1, Pallas kernels, body(): pl.pallas_call(kernel, out_shape=(jax.ShapeDtypeStruct((1, ROWS, LOADS),...  167 us

profile of v8, /device:TPU:1, one launch (start us, length us, event | category | flops | bytes accessed | tf_op | source)
XLA Modules:
  0.0 169.5 jit_solution(5199795129287014361)
XLA Ops:
  0.6 167.0 %shard_map.77 = (f32[1,256,128]{2,1,0:T(8,128)}, f32[1,256,128]{2,1,0:T(8,128)}, f32[256,128]{1,0:T(8,128)}, f32[256,128]{1,0:T(8,128)}) custom-call(f32[1,256,128]{2,1,0:T(8,128)} %rhs_hbm.1, f32[1,256]{1,0:T(1,128)} %diag_hbm.1, f32[1,192]{1,0:T(1,128)} %spring_hbm.1, bf16[1,256,2048]{2,1,0:T(8,128)(2,1)} %couple_hbm.1, bf16[256,4096]{1,0:T(8,128)(2,1)} %pre_hbm.1, ...), custom_call_target="tpu_custom_call" | custom-call | tf_op jit(solution)/shard_map/pallas_call | solution.py:338
  167.7 1.8 %bitcast_subtract_fusion = (f32[1,256,128]{2,1,0:T(8,128)}, f32[1,256,128]{2,1,0:T(8,128)}) fusion(f32[1,256,128]{2,1,0:T(8,128)} %get-tuple-element.8, f32[256,128]{1,0:T(8,128)} %get-tuple-element.9, f32[1,256,128]{2,1,0:T(8,128)} %get-tuple-element.6, f32[256,128]{1,0:T(8,128)} %get-tuple-element.7), kind=kLoop, calls=%fused_computation | loop fusion | flops 65536 | bytes 786432 | tf_op jit(solution)/shard_map/sub | solution.py:399

commit v9 on v8

--- a/solution.py
+++ b/solution.py
@@ -283,10 +283,9 @@
         for event in range(COLUMN):
             idx = take(rbuf, r_send, r_sem, event, COLUMN + 1 + event)
             qnew[idx] = pre_dot(idx)
-            if event == 3:
+            if event == 4:
                 dots_pair()
-            if event == 5:
-                dots_plane(turn)
+        dots_plane(turn)
         inverse[...] = 1.0 / ratio(dof_dots[:, 2, :], dof_dots[:, 1, :])
 
         def slope(idx, product):

time: 170 us -> 166 us (0.976)
  Pallas kernels: 167 us -> 163 us
    pallas_call x1, Pallas kernels: 167 us -> 163 us  [body(): pl.pallas_call(kernel, out_shape=(jax.ShapeDtypeStruct((1, ROWS, LOADS),...]
where the time goes in v9:
time: 166 us
  Pallas kernels  163 us (98%)
  other arithmetic  1.82 us (1%)
    pallas_call x1, Pallas kernels, body(): pl.pallas_call(kernel, out_shape=(jax.ShapeDtypeStruct((1, ROWS, LOADS),...  163 us

profile of v9, /device:TPU:1, one launch (start us, length us, event | category | flops | bytes accessed | tf_op | source)
XLA Modules:
  0.0 165.8 jit_solution(15240760685154764946)
XLA Ops:
  0.6 163.3 %shard_map.77 = (f32[1,256,128]{2,1,0:T(8,128)}, f32[1,256,128]{2,1,0:T(8,128)}, f32[256,128]{1,0:T(8,128)}, f32[256,128]{1,0:T(8,128)}) custom-call(f32[1,256,128]{2,1,0:T(8,128)} %rhs_hbm.1, f32[1,256]{1,0:T(1,128)} %diag_hbm.1, f32[1,192]{1,0:T(1,128)} %spring_hbm.1, bf16[1,256,2048]{2,1,0:T(8,128)(2,1)} %couple_hbm.1, bf16[256,4096]{1,0:T(8,128)(2,1)} %pre_hbm.1, ...), custom_call_target="tpu_custom_call" | custom-call | tf_op jit(solution)/shard_map/pallas_call | solution.py:337
  164.0 1.8 %bitcast_subtract_fusion = (f32[1,256,128]{2,1,0:T(8,128)}, f32[1,256,128]{2,1,0:T(8,128)}) fusion(f32[1,256,128]{2,1,0:T(8,128)} %get-tuple-element.8, f32[256,128]{1,0:T(8,128)} %get-tuple-element.9, f32[1,256,128]{2,1,0:T(8,128)} %get-tuple-element.6, f32[256,128]{1,0:T(8,128)} %get-tuple-element.7), kind=kLoop, calls=%fused_computation | loop fusion | flops 65536 | bytes 786432 | tf_op jit(solution)/shard_map/sub | solution.py:398
